TPU v7x, 32 devices: a whole 2x2x4 slice. The times are simulated.
32 devices in a mesh: tm: 4 (over x, core), particle: 2 (over y), cell: 4 (over z).
Axes of the slice: x: 2, y: 2, z: 4, core: 2. Of those that a mesh axis runs over, the one named last changes fastest.
Arguments:
- particles: float32 [4, 30, 2048], P('tm', None, 'particle'), may hold values from -50 to 50
- cell_points: float32 [4, 30, 4096], P('tm', None, 'cell'), may hold values from -50 to 50
- cell_counts: int32 [4], replicated, may hold values from 682 to 4096, as said below
- brownian: float32 [4, 30, 2048], P('tm', None, ('particle', 'cell')), may hold values from -6 to 6
Outputs:
- descent_direction: float32 [4, 30, 2048], P('tm', None, ('particle', 'cell'))
- updated_particles: float32 [4, 30, 2048], P('tm', None, ('particle', 'cell'))
Inputs may be any that keep to these rules, and one draw needn't show every extreme that they name: `cell_counts`: some time has all 4096 cells observed.
All inputs are finite; a program needn't handle non-finite values.
Results may differ from a plain program's by a relative error of at most 0.0003.
Values sent between devices are 32-bit elements; how exact they have to be, the bound alone decides.
No kernel may reach another device: no remote copies, remote signals or barrier semaphores. Data moves between devices by JAX's collectives and lax.ppermute only.
A program may use at most 64 MiB of HBM per device.

v0:
```python
import math

import jax
import jax.numpy as jnp
from jax import lax
from jax.sharding import PartitionSpec as P

DATA_VAR = 2.0
BRIDGE_VAR = 1.5
LANGEVIN_STRIDE = 0.05
NOISE_LEVEL = 1.0
lowest_score = -1e30


def joined(x, axis, combine):
    everything = jax.tree.map(lambda part: lax.all_gather(part, axis), x)
    first = jax.tree.map(lambda part: part[0], everything)

    def turn(k, so_far):
        return combine(so_far, jax.tree.map(lambda part: part[k], everything))

    return lax.fori_loop(1, lax.axis_size(axis), turn, first)


def passed_along(x, axis, by):
    count = lax.axis_size(axis)
    pairs = [(i, i + by) for i in range(count) if 0 <= i + by < count]
    return lax.ppermute(x, axis, pairs)


def fresh_state(feature_count, row_count):
    return (
        jnp.full((row_count,), lowest_score, jnp.float32),
        jnp.zeros((row_count,), jnp.float32),
        jnp.zeros((feature_count, row_count), jnp.float32),
    )


def fold_targets(running, queries, query_sq, targets, usable, spread):
    highest_seen, summed, weighted = running
    cross_terms = lax.dot_general(
        queries,
        targets,
        (((0,), (0,)), ((), ())),
        precision=lax.Precision.HIGHEST,
        preferred_element_type=jnp.float32,
    )
    scores = (2.0 * cross_terms - query_sq[:, None] - jnp.sum(targets * targets, 0)[None, :]) / (
        2.0 * spread
    )
    scores = jnp.where(usable[None, :], scores, lowest_score)
    new_high = jnp.maximum(highest_seen, jnp.max(scores, 1))
    factor = jnp.exp(highest_seen - new_high)
    expo_terms = jnp.where(usable[None, :], jnp.exp(scores - new_high[:, None]), 0.0)
    summed = summed * factor + jnp.sum(expo_terms, 1)
    weighted = weighted * factor[None, :] + lax.dot_general(
        targets,
        expo_terms,
        (((1,), (1,)), ((), ())),
        precision=lax.Precision.HIGHEST,
        preferred_element_type=jnp.float32,
    )
    return (new_high, summed, weighted)


def sweep(running, queries, query_sq, targets, spread, first_key, key_limit):
    key_span = math.gcd(targets.shape[1], 512)
    key_rounds = targets.shape[1] // key_span

    def visit(turn_index, carried):
        offset = turn_index * key_span
        key_block = lax.dynamic_slice_in_dim(targets, offset, key_span, 1)
        usable = first_key + offset + jnp.arange(key_span, dtype=jnp.int32) < key_limit
        return fold_targets(carried, queries, query_sq, key_block, usable, spread)

    return lax.fori_loop(0, key_rounds, visit, running)


def combine_parts(earlier_part, later_part):
    new_high = jnp.maximum(earlier_part[0], later_part[0])
    scale_first = jnp.exp(earlier_part[0] - new_high)
    scale_second = jnp.exp(later_part[0] - new_high)
    summed = earlier_part[1] * scale_first + later_part[1] * scale_second
    weighted = earlier_part[2] * scale_first[None, :] + later_part[2] * scale_second[None, :]
    return (new_high, summed, weighted)


def shards(particles, cell_points, cell_counts, brownian):
    own_block = particles[0]
    own_cells = cell_points[0]
    feature_count = own_block.shape[0]
    block_rows = own_block.shape[1]
    share_width = block_rows // lax.axis_size("cell")
    cell_index = lax.axis_index("cell")
    time_index = lax.axis_index("tm")
    share_start = cell_index * share_width
    local_portion = lax.dynamic_slice_in_dim(own_block, share_start, share_width, 1)
    cell_limit = jnp.sum(
        jnp.where(jnp.arange(cell_counts.shape[0], dtype=jnp.int32) == time_index, cell_counts, 0)
    )
    first_cell = cell_index * own_cells.shape[1]
    block_sq = jnp.sum(own_block * own_block, 0)
    starting = fresh_state(feature_count, block_rows)
    fit_state = sweep(starting, own_block, block_sq, own_cells, DATA_VAR, first_cell, cell_limit)
    fit_high, fit_sum, fit_weighted = joined(
        (fit_state[0], fit_state[1], fit_state[2]), "cell", combine_parts
    )
    share_sum = lax.dynamic_slice_in_dim(fit_sum, share_start, share_width, 0)
    share_weighted = lax.dynamic_slice_in_dim(fit_weighted, share_start, share_width, 1)
    fit_mean = share_weighted / share_sum[None, :]
    share_sq = jnp.sum(local_portion * local_portion, 0)
    share_start_state = fresh_state(feature_count, share_width)
    earlier = passed_along(own_block, "tm", 1)
    following = passed_along(own_block, "tm", -1)
    prior_piece = lax.all_gather(earlier, "particle", axis=1, tiled=True)
    later_piece = lax.all_gather(following, "particle", axis=1, tiled=True)
    prior_state = sweep(
        share_start_state, local_portion, share_sq, prior_piece, BRIDGE_VAR, 0, prior_piece.shape[1]
    )
    later_state = sweep(
        share_start_state, local_portion, share_sq, later_piece, BRIDGE_VAR, 0, later_piece.shape[1]
    )
    prior_mean = prior_state[2] / prior_state[1][None, :]
    later_mean = later_state[2] / later_state[1][None, :]
    has_prior = (time_index > 0).astype(jnp.float32)
    has_later = (time_index < lax.axis_size("tm") - 1).astype(jnp.float32)
    gradient = (local_portion - fit_mean) / DATA_VAR
    gradient = gradient + has_prior * (local_portion - prior_mean) / BRIDGE_VAR
    gradient = gradient + has_later * (local_portion - later_mean) / BRIDGE_VAR
    descent_direction = -gradient
    updated_particles = (
        local_portion
        + LANGEVIN_STRIDE * descent_direction
        + math.sqrt(2.0 * LANGEVIN_STRIDE * NOISE_LEVEL) * brownian[0]
    )
    return (descent_direction[None], updated_particles[None])


def solution(mesh):
    in_specs = (
        P("tm", None, "particle"),
        P("tm", None, "cell"),
        P(),
        P("tm", None, ("particle", "cell")),
    )
    out_specs = (P("tm", None, ("particle", "cell")), P("tm", None, ("particle", "cell")))
    return jax.shard_map(shards, mesh=mesh, in_specs=in_specs, out_specs=out_specs, check_vma=False)
```

profile of v0, /device:TPU:0, one launch (start us, length us, event | category | flops | bytes accessed | tf_op | source)
XLA Modules:
  0.0 88.7 jit_solution(13570196675577299496)
XLA Ops:
  0.6 1.6 %copy_bitcast_fusion = (f32[30,1024]{1,0:T(8,128)}, f32[30,1024]{1,0:T(8,128)S(1)}) fusion(f32[1,30,1024]{2,0,1:T(1,128)} %param.12, f32[1,30,1024]{2,0,1:T(1,128)} %param.13), kind=kLoop, calls=%fused_computation.76 | loop fusion | bytes 491520
  2.3 2.4 %collective-permute-start = (f32[30,1024]{1,0:T(8,128)}, f32[30,1024]{1,0:T(8,128)S(1)}, u32[]{:S(2)}, u32[]{:S(2)}) collective-permute-start(f32[30,1024]{1,0:T(8,128)} %get-tuple-element.1047), channel_id=1, source_target_pairs={{0,8},{8,16},{16,24},{1,9},{9,17},{17,25},{2,10},{10,18},{18,26},{... | collective-permute-start | bytes 368648 | tf_op jit(solution)/shard_map/ppermute | solution.py:28
  4.7 1.3 %collective-permute-start.1 = (f32[30,1024]{1,0:T(8,128)}, f32[30,1024]{1,0:T(8,128)S(1)}, u32[]{:S(2)}, u32[]{:S(2)}) collective-permute-start(f32[30,1024]{1,0:T(8,128)} %get-tuple-element.1047), channel_id=1, source_target_pairs={{8,0},{16,8},{24,16},{9,1},{17,9},{25,17},{10,2},{18,10},{26,18},{... | collective-permute-start | bytes 368648 | tf_op jit(solution)/shard_map/ppermute | solution.py:28
  6.0 0.9 %multiply_reduce_fusion.3 = f32[1024]{0:T(1024)S(1)} fusion(f32[1,30,1024]{2,0,1:T(1,128)} %param.12), kind=kLoop, calls=%fused_computation.78 | loop fusion | flops 60416 | bytes 126976 | tf_op jit(solution)/shard_map/reduce_sum | solution.py:102
  7.0 1.3 %fusion.43 = s32[]{:T(128)} fusion(s32[4]{0:T(128)} %param.14, s32[]{:T(128)S(6)} %axis_index.25), kind=kLoop, calls=%fused_computation.85 | loop fusion | flops 11 | bytes 24 | tf_op jit(solution)/shard_map/reduce_sum | solution.py:98
  8.2 11.5 %while.74 = (s32[]{:T(128)}, f32[1024]{0:T(1024)S(1)}, f32[1024]{0:T(1024)S(1)}, f32[30,1024]{1,0:T(8,128)S(1)}, s32[]{:T(128)}, /*index=5*/s32[]{:T(128)}, f32[...) while((s32[]{:T(128)}, f32[1024]{0:T(1024)S(1)}, ...), condition=%wide.region_6.7_spmd.clone, body=%wide.region_2.6_spmd.clone.sunk | while | flops 383383040 | bytes 6936791 | solution.py:76
  8.8 3.1 %fusion.72 = (f32[1024]{0:T(1024)S(1)}, f32[512,1024]{1,0:T(8,128)S(1)}) fusion(f32[512]{0:T(512)S(1)} %multiply_reduce_fusion.8, f32[1024]{0:T(1024)S(1)} %get-tuple-element.1074, f32[30,1024]{1,0:T(8,128)} %get-tuple-element.1073, f32[30,1024]{1,0:T(8,128)S(1)} %get-tuple-element.1072, s32[]{:T(128)S(6)} %select_n.136, ...), kind=kOutput, calls=%fused_computation.87.clone.1 | convolution fusion | flops 191888384 | bytes 2296324 | tf_op jit(solution)/shard_map/while/body/eval_jaxpr/dot_general | solution.py:41
  12.4 1.6 %fusion.75 = f32[30,1024]{1,0:T(8,128)S(1)} fusion(f32[512,1024]{1,0:T(8,128)S(1)} %get-tuple-element.949, f32[1024]{0:T(1024)S(1)} %select_maximum_fusion.2, pred[512]{0:T(512)(128)(4,1)S(1)} %add_compare_fusion.6, f32[30,1024]{1,0:T(8,128)S(1)} %get-tuple-element.1056, f32[1024]{0:T(1024)S(1)} %get-tuple-element.951, pred[]{:T(512)S(6)} %compare.9, ...), kind=kOutput, calls=%fused_computation.11.clone.1 | convolution fusion | flops 189884416 | bytes 2425349 | tf_op jit(solution)/shard_map/while/body/eval_jaxpr/dot_general | solution.py:56
  14.6 3.1 %fusion.72 = (f32[1024]{0:T(1024)S(1)}, f32[512,1024]{1,0:T(8,128)S(1)}) fusion(f32[512]{0:T(512)S(1)} %multiply_reduce_fusion.8, f32[1024]{0:T(1024)S(1)} %get-tuple-element.1074, f32[30,1024]{1,0:T(8,128)} %get-tuple-element.1073, f32[30,1024]{1,0:T(8,128)S(1)} %get-tuple-element.1072, s32[]{:T(128)S(6)} %select_n.136, ...), kind=kOutput, calls=%fused_computation.87.clone.1 | convolution fusion | flops 191888384 | bytes 2296324 | tf_op jit(solution)/shard_map/while/body/eval_jaxpr/dot_general | solution.py:41
  18.1 1.6 %fusion.75 = f32[30,1024]{1,0:T(8,128)S(1)} fusion(f32[512,1024]{1,0:T(8,128)S(1)} %get-tuple-element.949, f32[1024]{0:T(1024)S(1)} %select_maximum_fusion.2, pred[512]{0:T(512)(128)(4,1)S(1)} %add_compare_fusion.6, f32[30,1024]{1,0:T(8,128)S(1)} %get-tuple-element.1056, f32[1024]{0:T(1024)S(1)} %get-tuple-element.951, pred[]{:T(512)S(6)} %compare.9, ...), kind=kOutput, calls=%fused_computation.11.clone.1 | convolution fusion | flops 189884416 | bytes 2425349 | tf_op jit(solution)/shard_map/while/body/eval_jaxpr/dot_general | solution.py:56
  19.7 14.3 %all-gather = f32[4096]{0:T(1024)S(1)} all-gather(f32[1024]{0:T(1024)S(1)} %get-tuple-element.585), channel_id=2, replica_groups=mesh['tm'=4,'particle'=2,'cell'=4] {'cell'}, dimensions={0}, use_global_device_ids=true | all-gather | bytes 20480 | tf_op jit(solution)/shard_map/all_gather | solution.py:16
  34.0 13.2 %all-gather.1 = f32[4096]{0:T(1024)S(1)} all-gather(f32[1024]{0:T(1024)S(1)} %get-tuple-element.586), channel_id=3, replica_groups=mesh['tm'=4,'particle'=2,'cell'=4] {'cell'}, dimensions={0}, use_global_device_ids=true | all-gather | bytes 20480 | tf_op jit(solution)/shard_map/all_gather | solution.py:16
  47.3 15.9 %all-gather.3 = f32[4,30,1024]{2,1,0:T(8,128)S(1)} all-gather(f32[1,30,1024]{2,1,0:T(8,128)S(1)} %bitcast.42), channel_id=4, replica_groups=mesh['tm'=4,'particle'=2,'cell'=4] {'cell'}, dimensions={0}, use_global_device_ids=true | all-gather | bytes 614400 | tf_op jit(solution)/shard_map/all_gather | solution.py:16
  63.6 0.8 constant_dynamic-slice_fusion.2
  64.4 5.6 %all_gather.30 = f32[30,2048]{1,0:T(8,128)S(1)} all-gather(f32[30,1024]{1,0:T(8,128)S(1)} %collective-permute-done), channel_id=1, replica_groups=mesh['tm'=4,'particle'=2,'cell'=4] {'particle'}, dimensions={1}, use_global_device_ids=true | all-gather | bytes 368640 | tf_op jit(solution)/shard_map/all_gather | solution.py:115
  70.1 5.8 %while.75 = (s32[]{:T(128)}, f32[256]{0:T(256)S(1)}, f32[256]{0:T(256)S(1)}, f32[30,256]{1,0:T(8,128)S(1)}, f32[30,2048]{1,0:T(8,128)S(1)}, /*index=5*/f32[30,25...) while((s32[]{:T(128)}, f32[256]{0:T(256)S(1)}, ...), condition=%wide.region_14.15_spmd.clone, body=%wide.region_10.14_spmd.clone.sunk | while | flops 95869184 | bytes 1885367 | solution.py:76
  71.6 0.7 fusion.78
  73.0 0.7 fusion.78
  74.5 0.7 fusion.78
  75.9 5.6 %all_gather.31 = f32[30,2048]{1,0:T(8,128)S(1)} all-gather(f32[30,1024]{1,0:T(8,128)S(1)} %collective-permute-done.1), channel_id=1, replica_groups=mesh['tm'=4,'particle'=2,'cell'=4] {'particle'}, dimensions={1}, use_global_device_ids=true | all-gather | bytes 368640 | tf_op jit(solution)/shard_map/all_gather | solution.py:116
  81.5 5.8 %while.76 = (s32[]{:T(128)}, f32[256]{0:T(256)S(1)}, f32[256]{0:T(256)S(1)}, f32[30,256]{1,0:T(8,128)S(1)}, f32[30,2048]{1,0:T(8,128)S(1)}, /*index=5*/f32[30,25...) while((s32[]{:T(128)}, f32[256]{0:T(256)S(1)}, ...), condition=%wide.region_19.20_spmd.clone, body=%wide.region_15.19_spmd.clone.sunk | while | flops 95869184 | bytes 1885367 | solution.py:76
  81.6 0.7 fusion.84
  84.5 0.7 fusion.84
  85.9 0.7 fusion.84
  (104 shorter events, 11.0 us)
Async XLA Ops:
  2.3 62.2 %collective-permute-start = (f32[30,1024]{1,0:T(8,128)}, f32[30,1024]{1,0:T(8,128)S(1)}, u32[]{:S(2)}, u32[]{:S(2)}) collective-permute-start(f32[30,1024]{1,0:T(8,128)} %get-tuple-element.1047), channel_id=1, source_target_pairs={{0,8},{8,16},{16,24},{1,9},{9,17},{17,25},{2,10},{10,18},{18,26},{... | collective-permute-start | bytes 368648 | tf_op jit(solution)/shard_map/ppermute | solution.py:28
  4.7 71.2 %collective-permute-start.1 = (f32[30,1024]{1,0:T(8,128)}, f32[30,1024]{1,0:T(8,128)S(1)}, u32[]{:S(2)}, u32[]{:S(2)}) collective-permute-start(f32[30,1024]{1,0:T(8,128)} %get-tuple-element.1047), channel_id=1, source_target_pairs={{8,0},{16,8},{24,16},{9,1},{17,9},{25,17},{10,2},{18,10},{26,18},{... | collective-permute-start | bytes 368648 | tf_op jit(solution)/shard_map/ppermute | solution.py:28
  81.5 5.8 %copy-start = (f32[1,30,256]{2,0,1:T(1,128)S(1)}, f32[1,30,256]{2,0,1:T(1,128)}, u32[]{:S(2)}) copy-start(f32[1,30,256]{2,0,1:T(1,128)} %param.15) | copy-start | bytes 92164
where the time goes:
time: 90.3 us; the launch traced here: 88.7 us
  blocking collectives  54.7 us (61%)
  matrix products  18.9 us (21%)
  other arithmetic  6.14 us (7%)
  local copies, waits for them, and re-layouts  3.86 us (4%)
  starting transfers between devices  3.68 us (4%)
    all_gather x3, blocking collectives, joined(): everything = jax.tree.map(lambda part: lax.all_gather(part, axis), x)  43.4 us
    dot_general x10, matrix products, fold_targets(): lax.dot_general(queries, targets, (((0,), (0,)), ((), ())), precision=lax...  11.8 us
    dot_general x10, matrix products, fold_targets(): lax.dot_general(targets, expo_terms, (((1,), (1,)), ((), ())), precision=...  7.12 us
    all_gather x1, blocking collectives, shards(): later_piece = lax.all_gather(following, 'particle', axis=1, tiled=True)  5.64 us
    all_gather x1, blocking collectives, shards(): prior_piece = lax.all_gather(earlier, 'particle', axis=1, tiled=True)  5.64 us
    ppermute x2, starting transfers between devices, passed_along(): return lax.ppermute(x, axis, pairs)  3.68 us
    reduce_sum x10, other arithmetic, fold_targets(): summed = summed * factor + jnp.sum(expo_terms, 1)  1.97 us
  transfers between devices with their start and end apart: 2, of which 0 were waited for; matrix products, arithmetic and copies ran while one was open for 23% of the time, Pallas kernels for 0%

commit v1 on v0

v1 whole, which is shorter than its diff:
```python
import functools
import math

import jax
import jax.numpy as jnp
from jax import lax
from jax.experimental import pallas as pl
from jax.experimental.pallas import tpu as pltpu
from jax.sharding import PartitionSpec as P

DATA_VAR = 2.0
BRIDGE_VAR = 1.5
LANGEVIN_STRIDE = 0.05
NOISE_LEVEL = 1.0
LOWEST = -1e30
LANES = 128
GROUP = 32
FIT_SCALE = math.log2(math.e) / DATA_VAR
BRIDGE_SCALE = math.log2(math.e) / BRIDGE_VAR
f32, bf16 = jnp.float32, jnp.bfloat16


def load_columns(ref, features, first, count):
    blocks = ref.shape[0] // features
    return jnp.concatenate(
        [ref[pl.ds(first + k, features, stride=blocks), :] for k in range(count)], 1
    )


def three_parts(x):
    high = x.astype(bf16).astype(f32)
    rest = x - high
    middle = rest.astype(bf16).astype(f32)
    return high, middle, rest - middle


def grouped(x, first, second):
    return jnp.concatenate([x, first, second], 0)


def target_operand(x, scale, usable=None):
    width = x.shape[1]
    zero, one = jnp.zeros((1, width), f32), jnp.ones((1, width), f32)
    norm_high, norm_middle, norm_low = three_parts(-0.5 * scale * jnp.sum(x * x, 0, keepdims=True))
    if usable is not None:
        norm_high = jnp.where(usable, norm_high, LOWEST)
        norm_middle = jnp.where(usable, norm_middle, 0.0)
        norm_low = jnp.where(usable, norm_low, 0.0)
    high, middle, low = three_parts(x)
    return jnp.concatenate(
        [
            grouped(high, norm_high, norm_middle),
            grouped(middle, norm_low, zero),
            grouped(high, one, zero),
            grouped(low, zero, zero),
            grouped(middle, zero, zero),
            grouped(high, zero, zero),
        ],
        0,
    ).astype(bf16)


def query_operand(x, scale):
    width = x.shape[1]
    zero, one = jnp.zeros((1, width), f32), jnp.ones((1, width), f32)
    high, middle, low = three_parts(x * scale)
    return (
        jnp.concatenate(
            [
                grouped(high, one, one),
                grouped(high, one, zero),
                grouped(middle, zero, zero),
                grouped(high, zero, zero),
                grouped(middle, zero, zero),
                grouped(low, zero, zero),
            ],
            0,
        )
        .astype(bf16)
        .T
    )


def partial_sums(queries, targets):
    scores = jnp.dot(queries, targets, preferred_element_type=f32)
    highest = jnp.max(scores, 1, keepdims=True)
    weights = jnp.exp2(scores - highest)
    weights_high = weights.astype(bf16)
    weights_low = (weights - weights_high.astype(f32)).astype(bf16)
    values = targets[2 * GROUP : 5 * GROUP]
    along = (((1,), (1,)), ((), ()))
    sums = lax.dot_general(weights_high, values, along, preferred_element_type=f32)
    sums = sums + lax.dot_general(weights_low, values, along, preferred_element_type=f32)
    column = lax.broadcasted_iota(jnp.int32, sums.shape, 1)
    turned = jnp.where(column == GROUP - 1, highest, sums).T
    return turned[:GROUP] + turned[GROUP : 2 * GROUP] + turned[2 * GROUP : 3 * GROUP]


def merged(parts):
    if len(parts) == 1:
        return parts[0]
    highest = functools.reduce(jnp.maximum, [part[GROUP - 1 :] for part in parts])
    total = sum(part * jnp.exp2(part[GROUP - 1 :] - highest) for part in parts)
    row = lax.broadcasted_iota(jnp.int32, total.shape, 0)
    return jnp.where(row == GROUP - 1, highest, total)


def mean_of(part):
    return part / part[GROUP - 2 : GROUP - 1]


def usable_cells(counts_ref, which, width):
    count = counts_ref[lax.axis_index("tm")]
    position = which * width + lax.broadcasted_iota(jnp.int32, (1, width), 1)
    return position < count


def fit_own(features, halves, counts_ref, block_ref, cells_ref, parts_ref, queries_ref):
    me = lax.axis_index("cell")
    share = parts_ref.shape[2]
    per_share = share // LANES
    columns = [
        load_columns(block_ref, features, lax.bitwise_xor(me, 2 * j) * per_share, per_share)
        for j in range(halves)
    ]
    queries = query_operand(jnp.concatenate(columns, 1), FIT_SCALE)
    queries_ref[...] = queries
    blocks = cells_ref.shape[0] // features
    targets = target_operand(
        load_columns(cells_ref, features, 0, blocks),
        FIT_SCALE,
        usable_cells(counts_ref, me, blocks * LANES),
    )
    parts = partial_sums(queries, targets)
    for j in range(halves):
        parts_ref[j] = parts[:, j * share : (j + 1) * share]


def fit_next(features, halves, counts_ref, queries_ref, cells_ref, parts_ref, *out_refs):
    other = lax.bitwise_xor(lax.axis_index("cell"), 1)
    share = parts_ref.shape[2]
    blocks = cells_ref.shape[0] // features
    targets = target_operand(
        load_columns(cells_ref, features, 0, blocks),
        FIT_SCALE,
        usable_cells(counts_ref, other, blocks * LANES),
    )
    parts = partial_sums(queries_ref[...], targets)
    for j in range(halves):
        out_refs[j][...] = merged([parts_ref[j], parts[:, j * share : (j + 1) * share]])


def bridges(features, sides, block_ref, *refs):
    *key_refs, out_ref = refs
    share = out_ref.shape[1]
    per_share = share // LANES
    x = load_columns(block_ref, features, lax.axis_index("cell") * per_share, per_share)
    queries = query_operand(x, BRIDGE_SCALE)
    time, times = lax.axis_index("tm"), lax.axis_size("tm")
    odd = lax.rem(time, 2)
    pull = jnp.zeros((features, share), f32)
    per_side = len(key_refs) // sides
    for side in range(sides):
        parts = []
        for key_ref in key_refs[side * per_side : (side + 1) * per_side]:
            blocks = key_ref.shape[0] // features
            targets = target_operand(load_columns(key_ref, features, 0, blocks), BRIDGE_SCALE)
            parts.append(partial_sums(queries, targets))
        partner = time + 1 - 2 * odd if side == 0 else time - 1 + 2 * odd
        there = jnp.logical_and(partner >= 0, partner < times)
        mean = mean_of(merged(parts))[:features]
        pull = pull + jnp.where(there, (x - mean) / BRIDGE_VAR, 0.0)
    out_ref[:features, :] = pull


def finish(features, block_ref, noise_ref, pull_ref, *refs):
    *part_refs, drift_ref, moved_ref = refs
    share = pull_ref.shape[1]
    per_share = share // LANES
    first = lax.axis_index("cell") * per_share
    mean = mean_of(merged([ref[...] for ref in part_refs]))
    for k in range(per_share):
        lanes = slice(k * LANES, (k + 1) * LANES)
        rows = pl.ds(k, features, stride=per_share)
        x = block_ref[pl.ds(first + k, features, stride=block_ref.shape[0] // features), :]
        gradient = (x - mean[:features, lanes]) / DATA_VAR + pull_ref[:features, lanes]
        drift = -gradient
        drift_ref[rows, :] = drift
        moved_ref[rows, :] = (
            x
            + LANGEVIN_STRIDE * drift
            + math.sqrt(2.0 * LANGEVIN_STRIDE * NOISE_LEVEL) * noise_ref[rows, :]
        )


VMEM = pl.BlockSpec(memory_space=pltpu.VMEM)
SMEM = pl.BlockSpec(memory_space=pltpu.SMEM)


def call(kernel, out_shape, in_specs, args, flops, out_specs=None):
    out_specs = jax.tree.map(lambda _: VMEM, out_shape) if out_specs is None else out_specs
    return pl.pallas_call(
        kernel,
        out_shape=out_shape,
        in_specs=in_specs,
        out_specs=out_specs,
        compiler_params=pltpu.CompilerParams(vmem_limit_bytes=24 * 1024 * 1024),
        cost_estimate=pl.CostEstimate(
            flops=flops, bytes_accessed=4 * sum(a.size for a in args), transcendentals=0
        ),
    )(*args)


def swaps(mesh_sizes, time_of, particle_shift):
    times, blocks = mesh_sizes
    pairs = []
    for t in range(times):
        if 0 <= time_of(t) < times:
            for p in range(blocks):
                pairs.append((t * blocks + p, time_of(t) * blocks + (p + particle_shift) % blocks))
    return pairs


def shards(particles, cell_points, cell_counts, brownian):
    features = particles.shape[1]
    block = particles.reshape(-1, LANES)
    cells = cell_points.reshape(-1, LANES)
    noise = brownian.reshape(-1, LANES)
    share = brownian.shape[2]
    cell_count, halves = lax.axis_size("cell"), lax.axis_size("cell") // 2
    sizes = (lax.axis_size("tm"), lax.axis_size("particle"))

    def over_cell(x, by):
        return lax.ppermute(x, "cell", [(c, c ^ by) for c in range(cell_count)])

    next_cells = over_cell(cells, 1)
    keys = []
    for time_of in (lambda t: t ^ 1, lambda t: t - 1 if t % 2 == 0 else t + 1):
        for shift in range(sizes[1]):
            keys.append(lax.ppermute(block, ("tm", "particle"), swaps(sizes, time_of, shift)))

    part = jax.ShapeDtypeStruct((GROUP, share), f32)
    parts, queries = call(
        functools.partial(fit_own, features, halves),
        (
            jax.ShapeDtypeStruct((halves, GROUP, share), f32),
            jax.ShapeDtypeStruct((halves * share, 6 * GROUP), bf16),
        ),
        [SMEM, VMEM, VMEM],
        (cell_counts, block, cells),
        10**9,
    )
    own, *others = call(
        functools.partial(fit_next, features, halves),
        (part,) * halves,
        [SMEM, VMEM, VMEM, VMEM],
        (cell_counts, queries, next_cells, parts),
        10**9,
    )
    arrived = [over_cell(other, 2 * (j + 1)) for j, other in enumerate(others)]
    pull = call(
        functools.partial(bridges, features, 2),
        part,
        [VMEM] * (1 + len(keys)),
        (block, *keys),
        3 * 10**9,
    )
    out = jax.ShapeDtypeStruct(noise.shape, f32)
    drift, moved = call(
        functools.partial(finish, features),
        (out, out),
        [VMEM] * (4 + len(arrived)),
        (block, noise, pull, own, *arrived),
        10**6,
        out_specs=(pl.BlockSpec(noise.shape, lambda: (0, 0)),) * 2,
    )
    return drift.reshape(brownian.shape), moved.reshape(brownian.shape)


def solution(mesh):
    in_specs = (
        P("tm", None, "particle"),
        P("tm", None, "cell"),
        P(),
        P("tm", None, ("particle", "cell")),
    )
    out_specs = (P("tm", None, ("particle", "cell")), P("tm", None, ("particle", "cell")))
    return jax.shard_map(shards, mesh=mesh, in_specs=in_specs, out_specs=out_specs, check_vma=False)
```

time: 90.3 us -> 23.4 us (0.26)
  the two profiles are of different devices: /device:TPU:0 before, /device:TPU:1 now
where the time goes in v1:
time: 23.4 us; the launch traced here: 23.3 us
  starting transfers between devices  12.1 us (52%)
  Pallas kernels  7.16 us (31%)
  local copies, waits for them, and re-layouts  3.1 us (13%)
  between operations  0.77 us (3%)
    ppermute x4, starting transfers between devices, shards(): lax.ppermute(block, ('tm', 'particle'), swaps(sizes, time_of, shift))  7.58 us
    pallas_call x4, Pallas kernels, call(): pl.pallas_call(kernel, out_shape=out_shape, in_specs=in_specs, out_specs=...  7.16 us
    ppermute x2, starting transfers between devices, over_cell(): return lax.ppermute(x, 'cell', [(c, c ^ by) for c in range(cell_count)])  4.56 us
    unnamed x10, local copies, waits for them, and re-layouts  1.81 us
    reshape x2, local copies, waits for them, and re-layouts, shards(): return (drift.reshape(brownian.shape), moved.reshape(brownian.shape))  1.28 us
  transfers between devices with their start and end apart: 6, of which 0 were waited for; matrix products, arithmetic and copies ran while one was open for 0% of the time, Pallas kernels for 31%

profile of v1, /device:TPU:1, one launch (start us, length us, event | category | flops | bytes accessed | tf_op | source)
XLA Modules:
  0.0 23.3 jit_solution(8106674298411576167)
XLA Ops:
  0.6 2.2 %collective-permute-start.4 = (f32[240,128]{1,0:T(8,128)}, f32[240,128]{1,0:T(8,128)S(1)}, u32[]{:S(2)}, u32[]{:S(2)}) collective-permute-start(f32[240,128]{1,0:T(8,128)} %bitcast.9), channel_id=1, source_target_pairs={{0,1},{1,0},{2,3},{3,2},{4,5},{5,4},{6,7},{7,6},{8,9},{9,8},{10,11... | collective-permute-start | bytes 368648 | tf_op jit(solution)/shard_map/ppermute | solution.py:234
  2.8 1.0 %collective-permute-start = (f32[240,128]{1,0:T(8,128)}, f32[240,128]{1,0:T(8,128)S(1)}, u32[]{:S(2)}, u32[]{:S(2)}) collective-permute-start(f32[240,128]{1,0:T(8,128)} %bitcast.2), channel_id=1, source_target_pairs={{0,8},{4,12},{8,0},{12,4},{16,24},{20,28},{24,16},{28,20},{1,9},{5... | collective-permute-start | bytes 368648 | tf_op jit(solution)/shard_map/ppermute | solution.py:240
  3.8 1.1 %collective-permute-start.1 = (f32[240,128]{1,0:T(8,128)}, f32[240,128]{1,0:T(8,128)S(1)}, u32[]{:S(2)}, u32[]{:S(2)}) collective-permute-start(f32[240,128]{1,0:T(8,128)} %bitcast.3), channel_id=1, source_target_pairs={{0,12},{4,8},{8,4},{12,0},{16,28},{20,24},{24,20},{28,16},{1,13},{... | collective-permute-start | bytes 368648 | tf_op jit(solution)/shard_map/ppermute | solution.py:240
  4.9 3.5 %collective-permute-start.2 = (f32[240,128]{1,0:T(8,128)}, f32[240,128]{1,0:T(8,128)S(1)}, u32[]{:S(2)}, u32[]{:S(2)}) collective-permute-start(f32[240,128]{1,0:T(8,128)} %bitcast.4), channel_id=1, source_target_pairs={{8,16},{12,20},{16,8},{20,12},{9,17},{13,21},{17,9},{21,13},{10,18... | collective-permute-start | bytes 368648 | tf_op jit(solution)/shard_map/ppermute | solution.py:240
  8.4 2.0 %collective-permute-start.3 = (f32[240,128]{1,0:T(8,128)}, f32[240,128]{1,0:T(8,128)S(1)}, u32[]{:S(2)}, u32[]{:S(2)}) collective-permute-start(f32[240,128]{1,0:T(8,128)} %bitcast.5), channel_id=1, source_target_pairs={{8,20},{12,16},{16,12},{20,8},{9,21},{13,17},{17,13},{21,9},{10,22... | collective-permute-start | bytes 368648 | tf_op jit(solution)/shard_map/ppermute | solution.py:240
  10.4 0.0 copy-start
  10.4 0.9 %copy-done = f32[1,30,1024]{2,0,1:T(1,128)S(1)} copy-done((f32[1,30,1024]{2,0,1:T(1,128)S(1)}, f32[1,30,1024]{2,0,1:T(1,128)}, u32[]{:S(2)}) %copy-start) | copy-done | bytes 122904
  11.3 0.9 %copy-done.2 = f32[1,30,1024]{2,0,1:T(1,128)S(1)} copy-done((f32[1,30,1024]{2,0,1:T(1,128)S(1)}, f32[1,30,1024]{2,0,1:T(1,128)}, u32[]{:S(2)}) %copy-start.2) | copy-done | bytes 122904
  12.2 2.3 %shard_map.60 = (f32[2,32,256]{2,1,0:T(8,128)S(1)}, bf16[512,192]{1,0:T(8,128)(2,1)S(1)}) custom-call(s32[4]{0:T(128)S(1)} %copy-done.3, f32[240,128]{1,0:T(8,128)S(1)} %bitcast.6, f32[240,128]{1,0:T(8,128)S(1)} %bitcast.10), custom_call_target="tpu_custom_call" | custom-call | flops 1000000000 | bytes 245776 | tf_op jit(solution)/shard_map/pallas_call | solution.py:202
  14.5 0.0 copy-done.4
  14.6 0.1 reduce
  14.7 0.0 collective-permute-done.4.cells_ref
  14.7 0.0 copy-start.1
  14.7 2.3 %shard_map.61 = (f32[32,256]{1,0:T(8,128)S(1)}, f32[32,256]{1,0:T(8,128)S(1)}) custom-call(s32[4]{0:T(128)S(1)} %copy-done.3, bf16[512,192]{1,0:T(8,128)(2,1)S(1)} %get-tuple-element.8.queries_ref, f32[240,128]{1,0:T(8,128)S(1)} %collective-permute-done.4.cells_ref, f32[2,32,256]{2,1,0:T(8,128)S(1)} %get-tuple-element.9.parts_ref), custom_call_target="tpu_custom_call" | custom-call | flops 1000000000 | bytes 581648 | tf_op jit(solution)/shard_map/pallas_call | solution.py:202
  17.0 2.4 %collective-permute-start.5 = (f32[32,256]{1,0:T(8,128)S(1)}, f32[32,256]{1,0:T(8,128)S(1)}, u32[]{:S(2)}, u32[]{:S(2)}) collective-permute-start(f32[32,256]{1,0:T(8,128)S(1)} %get-tuple-element.11), channel_id=1, source_target_pairs={{0,2},{1,3},{2,0},{3,1},{4,6},{5,7},{6,4},{7,5},{8,10},{9,11},{10,... | collective-permute-start | bytes 98312 | tf_op jit(solution)/shard_map/ppermute | solution.py:234
  19.3 0.0 collective-permute-done.refs_0_
  19.3 0.0 collective-permute-done.1.refs_1_
  19.3 0.0 collective-permute-done.2.refs_2_
  19.4 0.0 collective-permute-done.3.refs_3_
  19.4 0.0 copy-done.1
  19.4 2.5 %shard_map.59.pull_ref = f32[32,256]{1,0:T(8,128)S(1)} custom-call(f32[240,128]{1,0:T(8,128)S(1)} %bitcast.7, f32[240,128]{1,0:T(8,128)S(1)} %collective-permute-done.refs_0_, f32[240,128]{1,0:T(8,128)S(1)} %collective-permute-done.1.refs_1_, f32[240,128]{1,0:T(8,128)S(1)} %collective-permute-done.2.refs_2_, f32[240,128]{1,0:T(8,128)S(1)} %collective-permute-done.3.refs_3_), custom_call_target="tpu_custom_call" | custom-call | flops 3000000000 | bytes 614400 | tf_op jit(solution)/shard_map/pallas_call | solution.py:202
  21.9 0.0 collective-permute-done.5.refs_1_
  22.0 0.6 %reshape.24 = f32[1,30,256]{2,0,1:T(1,128)} reshape(f32[60,128]{1,0:T(8,128)S(1)} %get-tuple-element.12) | data formatting | bytes 61440 | tf_op jit(solution)/shard_map/reshape | solution.py:277
  22.6 0.6 %reshape.25 = f32[1,30,256]{2,0,1:T(1,128)} reshape(f32[60,128]{1,0:T(8,128)S(1)} %get-tuple-element.13) | data formatting | bytes 61440 | tf_op jit(solution)/shard_map/reshape | solution.py:277
  (6 shorter events, 0.0 us)
Async XLA Ops:
  0.6 9.8 %copy-start.3 = (s32[4]{0:T(128)S(1)}, s32[4]{0:T(128)}, u32[]{:S(2)}) copy-start(s32[4]{0:T(128)} %counts_ref.3) | copy-start | bytes 52
  0.6 14.0 %collective-permute-start.4 = (f32[240,128]{1,0:T(8,128)}, f32[240,128]{1,0:T(8,128)S(1)}, u32[]{:S(2)}, u32[]{:S(2)}) collective-permute-start(f32[240,128]{1,0:T(8,128)} %bitcast.9), channel_id=1, source_target_pairs={{0,1},{1,0},{2,3},{3,2},{4,5},{5,4},{6,7},{7,6},{8,9},{9,8},{10,11... | collective-permute-start | bytes 368648 | tf_op jit(solution)/shard_map/ppermute | solution.py:234
  2.8 16.5 %collective-permute-start = (f32[240,128]{1,0:T(8,128)}, f32[240,128]{1,0:T(8,128)S(1)}, u32[]{:S(2)}, u32[]{:S(2)}) collective-permute-start(f32[240,128]{1,0:T(8,128)} %bitcast.2), channel_id=1, source_target_pairs={{0,8},{4,12},{8,0},{12,4},{16,24},{20,28},{24,16},{28,20},{1,9},{5... | collective-permute-start | bytes 368648 | tf_op jit(solution)/shard_map/ppermute | solution.py:240
  3.8 15.6 %collective-permute-start.1 = (f32[240,128]{1,0:T(8,128)}, f32[240,128]{1,0:T(8,128)S(1)}, u32[]{:S(2)}, u32[]{:S(2)}) collective-permute-start(f32[240,128]{1,0:T(8,128)} %bitcast.3), channel_id=1, source_target_pairs={{0,12},{4,8},{8,4},{12,0},{16,28},{20,24},{24,20},{28,16},{1,13},{... | collective-permute-start | bytes 368648 | tf_op jit(solution)/shard_map/ppermute | solution.py:240
  4.9 14.4 %collective-permute-start.2 = (f32[240,128]{1,0:T(8,128)}, f32[240,128]{1,0:T(8,128)S(1)}, u32[]{:S(2)}, u32[]{:S(2)}) collective-permute-start(f32[240,128]{1,0:T(8,128)} %bitcast.4), channel_id=1, source_target_pairs={{8,16},{12,20},{16,8},{20,12},{9,17},{13,21},{17,9},{21,13},{10,18... | collective-permute-start | bytes 368648 | tf_op jit(solution)/shard_map/ppermute | solution.py:240
  8.4 10.9 %collective-permute-start.3 = (f32[240,128]{1,0:T(8,128)}, f32[240,128]{1,0:T(8,128)S(1)}, u32[]{:S(2)}, u32[]{:S(2)}) collective-permute-start(f32[240,128]{1,0:T(8,128)} %bitcast.5), channel_id=1, source_target_pairs={{8,20},{12,16},{16,12},{20,8},{9,21},{13,17},{17,13},{21,9},{10,22... | collective-permute-start | bytes 368648 | tf_op jit(solution)/shard_map/ppermute | solution.py:240
  10.4 0.9 %copy-start = (f32[1,30,1024]{2,0,1:T(1,128)S(1)}, f32[1,30,1024]{2,0,1:T(1,128)}, u32[]{:S(2)}) copy-start(f32[1,30,1024]{2,0,1:T(1,128)} %param.4) | copy-start | bytes 368644
  11.3 0.9 %copy-start.2 = (f32[1,30,1024]{2,0,1:T(1,128)S(1)}, f32[1,30,1024]{2,0,1:T(1,128)}, u32[]{:S(2)}) copy-start(f32[1,30,1024]{2,0,1:T(1,128)} %param.5) | copy-start | bytes 368644
  12.2 2.3 %copy-start.4 = (f32[1,30,256]{2,0,1:T(1,128)S(1)}, f32[1,30,256]{2,0,1:T(1,128)}, u32[]{:S(2)}) copy-start(f32[1,30,256]{2,0,1:T(1,128)} %param.7) | copy-start | bytes 92164
  14.7 4.7 %copy-start.1 = (f32[1,30,1024]{2,0,1:T(1,128)S(1)}, f32[1,30,1024]{2,0,1:T(1,128)}, u32[]{:S(2)}) copy-start(f32[1,30,1024]{2,0,1:T(1,128)} %param.4) | copy-start | bytes 368644
  17.0 5.0 %collective-permute-start.5 = (f32[32,256]{1,0:T(8,128)S(1)}, f32[32,256]{1,0:T(8,128)S(1)}, u32[]{:S(2)}, u32[]{:S(2)}) collective-permute-start(f32[32,256]{1,0:T(8,128)S(1)} %get-tuple-element.11), channel_id=1, source_target_pairs={{0,2},{1,3},{2,0},{3,1},{4,6},{5,7},{6,4},{7,5},{8,10},{9,11},{10,... | collective-permute-start | bytes 98312 | tf_op jit(solution)/shard_map/ppermute | solution.py:234

commit v2 on v1

v2 whole, which is shorter than its diff:
```python
import functools
import math

import jax
import jax.numpy as jnp
from jax import lax
from jax.experimental import pallas as pl
from jax.experimental.pallas import tpu as pltpu
from jax.sharding import PartitionSpec as P

DATA_VAR = 2.0
BRIDGE_VAR = 1.5
LANGEVIN_STRIDE = 0.05
NOISE_LEVEL = 1.0
LOWEST = -1e30
LANES = 128
GROUP = 32
FIT_SCALE = math.log2(math.e) / DATA_VAR
BRIDGE_SCALE = math.log2(math.e) / BRIDGE_VAR
f32, bf16 = jnp.float32, jnp.bfloat16


def load_columns(ref, features, first, count):
    blocks = ref.shape[0] // features
    return jnp.concatenate(
        [ref[pl.ds(first + k, features, stride=blocks), :] for k in range(count)], 1
    )


def three_parts(x):
    high = x.astype(bf16).astype(f32)
    rest = x - high
    middle = rest.astype(bf16).astype(f32)
    return high, middle, rest - middle


def grouped(x, first, second):
    return jnp.concatenate([x, first, second], 0)


def target_operand(x, scale, usable=None):
    width = x.shape[1]
    zero, one = jnp.zeros((1, width), f32), jnp.ones((1, width), f32)
    norm_high, norm_middle, norm_low = three_parts(-0.5 * scale * jnp.sum(x * x, 0, keepdims=True))
    if usable is not None:
        norm_high = jnp.where(usable, norm_high, LOWEST)
        norm_middle = jnp.where(usable, norm_middle, 0.0)
        norm_low = jnp.where(usable, norm_low, 0.0)
    high, middle, low = three_parts(x)
    return jnp.concatenate(
        [
            grouped(high, norm_high, norm_middle),
            grouped(middle, norm_low, zero),
            grouped(high, one, zero),
            grouped(low, zero, zero),
            grouped(middle, zero, zero),
            grouped(high, zero, zero),
        ],
        0,
    ).astype(bf16)


def query_operand(x, scale):
    width = x.shape[1]
    zero, one = jnp.zeros((1, width), f32), jnp.ones((1, width), f32)
    high, middle, low = three_parts(x * scale)
    return (
        jnp.concatenate(
            [
                grouped(high, one, one),
                grouped(high, one, zero),
                grouped(middle, zero, zero),
                grouped(high, zero, zero),
                grouped(middle, zero, zero),
                grouped(low, zero, zero),
            ],
            0,
        )
        .astype(bf16)
        .T
    )


def partial_sums(queries, targets):
    scores = jnp.dot(queries, targets, preferred_element_type=f32)
    highest = jnp.max(scores, 1, keepdims=True)
    weights = jnp.exp2(scores - highest)
    weights_high = weights.astype(bf16)
    weights_low = (weights - weights_high.astype(f32)).astype(bf16)
    values = targets[2 * GROUP : 5 * GROUP]
    along = (((1,), (1,)), ((), ()))
    sums = lax.dot_general(weights_high, values, along, preferred_element_type=f32)
    sums = sums + lax.dot_general(weights_low, values, along, preferred_element_type=f32)
    column = lax.broadcasted_iota(jnp.int32, sums.shape, 1)
    turned = jnp.where(column == GROUP - 1, highest, sums).T
    return turned[:GROUP] + turned[GROUP : 2 * GROUP] + turned[2 * GROUP : 3 * GROUP]


def merged(parts):
    if len(parts) == 1:
        return parts[0]
    highest = functools.reduce(jnp.maximum, [part[GROUP - 1 :] for part in parts])
    total = sum(part * jnp.exp2(part[GROUP - 1 :] - highest) for part in parts)
    row = lax.broadcasted_iota(jnp.int32, total.shape, 0)
    return jnp.where(row == GROUP - 1, highest, total)


def mean_of(part):
    return part / part[GROUP - 2 : GROUP - 1]


def usable_cells(counts_ref, positions_ref, which):
    count = counts_ref[lax.axis_index("tm")]
    return positions_ref[0:1, :] + which * positions_ref.shape[1] < count


def own_cell():
    return lax.axis_index("cell")


def share_columns(ref, features, which, share):
    blocks = share // LANES
    return load_columns(ref, features, which * blocks, blocks)


def whole(ref, features):
    return load_columns(ref, features, 0, ref.shape[0] // features)


def number_cells(positions_ref):
    positions_ref[...] = lax.broadcasted_iota(jnp.int32, positions_ref.shape, 1)


def fit_first(features, share, counts_ref, positions_ref, block_ref, cells_ref, *refs):
    parts_ref, queries_ref, operand_ref = refs
    columns = [
        share_columns(block_ref, features, lax.bitwise_xor(own_cell(), 2 * (j + 1)), share)
        for j in range(parts_ref.shape[0])
    ]
    queries = query_operand(jnp.concatenate(columns, 1), FIT_SCALE)
    queries_ref[...] = queries
    usable = usable_cells(counts_ref, positions_ref, own_cell())
    targets = target_operand(whole(cells_ref, features), FIT_SCALE, usable)
    operand_ref[...] = targets
    parts = partial_sums(queries, targets)
    for j in range(parts_ref.shape[0]):
        parts_ref[j] = parts[:, j * share : (j + 1) * share]


def fit_second(features, share, counts_ref, positions_ref, queries_ref, parts_ref, *refs):
    cells_ref, operand_ref, *fit_refs = refs
    usable = usable_cells(counts_ref, positions_ref, lax.bitwise_xor(own_cell(), 1))
    targets = target_operand(whole(cells_ref, features), FIT_SCALE, usable)
    operand_ref[...] = targets
    parts = partial_sums(queries_ref[...], targets)
    for j, fit_ref in enumerate(fit_refs):
        fit_ref[...] = merged([parts_ref[j], parts[:, j * share : (j + 1) * share]])


def bridge_others(features, share, blocks, *refs):
    side_refs, other_refs = refs[:2], refs[2 : 1 + blocks]
    operand_refs, pull_refs = refs[1 + blocks : 3 + blocks], refs[3 + blocks :]
    queries = query_operand(
        jnp.concatenate([share_columns(r, features, own_cell(), share) for r in other_refs], 1),
        BRIDGE_SCALE,
    )
    for side, (side_ref, operand_ref) in enumerate(zip(side_refs, operand_refs)):
        targets = target_operand(whole(side_ref, features), BRIDGE_SCALE)
        operand_ref[...] = targets
        parts = partial_sums(queries, targets)
        for j, pull_ref in enumerate(pull_refs):
            pull_ref[side * GROUP : (side + 1) * GROUP, :] = parts[:, j * share : (j + 1) * share]


def for_own(features, share, block_ref, *refs):
    own_ref, near_ref, *side_refs = refs[:4]
    fit_ref, pull_ref = refs[4:]
    x = share_columns(block_ref, features, own_cell(), share)
    queries = query_operand(x, FIT_SCALE)
    fit_ref[...] = merged([partial_sums(queries, ref[...]) for ref in (own_ref, near_ref)])
    queries = query_operand(x, BRIDGE_SCALE)
    for side, side_ref in enumerate(side_refs):
        pull_ref[side * GROUP : (side + 1) * GROUP, :] = partial_sums(queries, side_ref[...])


def finish(features, share, blocks, block_ref, noise_ref, *refs):
    pull_refs, fit_refs = refs[:blocks], refs[blocks:-5]
    drift_out, moved_out, drift_ref, moved_ref, sem = refs[-5:]
    per_share = share // LANES
    first = own_cell() * per_share
    time, times = lax.axis_index("tm"), lax.axis_size("tm")
    step = 1 - 2 * lax.rem(time, 2)
    fit_mean = mean_of(merged([ref[...] for ref in fit_refs]))
    side_means = [
        mean_of(merged([ref[side * GROUP : (side + 1) * GROUP, :] for ref in pull_refs]))
        for side in range(2)
    ]
    partners = [time + step, time - step]
    there = [jnp.logical_and(other >= 0, other < times) for other in partners]
    for k in range(per_share):
        lanes = slice(k * LANES, (k + 1) * LANES)
        x = block_ref[pl.ds(first + k, features, stride=block_ref.shape[0] // features), :]
        gradient = (x - fit_mean[:features, lanes]) / DATA_VAR
        for mean, present in zip(side_means, there):
            gradient = gradient + jnp.where(present, (x - mean[:features, lanes]) / BRIDGE_VAR, 0.0)
        drift = -gradient
        drift_ref[:, 0, lanes] = drift
        moved_ref[:, 0, lanes] = (
            x
            + LANGEVIN_STRIDE * drift
            + math.sqrt(2.0 * LANGEVIN_STRIDE * NOISE_LEVEL) * noise_ref[:, 0, lanes]
        )
    copies = [
        pltpu.make_async_copy(drift_ref, drift_out, sem.at[0]),
        pltpu.make_async_copy(moved_ref, moved_out, sem.at[1]),
    ]
    for copy in copies:
        copy.start()
    for copy in copies:
        copy.wait()


VMEM = pl.BlockSpec(memory_space=pltpu.VMEM)
SMEM = pl.BlockSpec(memory_space=pltpu.SMEM)


def call(kernel, out_shape, args, flops, counts=False, out_spec=VMEM, scratch=()):
    return pl.pallas_call(
        kernel,
        out_shape=out_shape,
        in_specs=[SMEM if counts and k == 0 else VMEM for k in range(len(args))],
        out_specs=jax.tree.map(lambda _: out_spec, out_shape),
        scratch_shapes=scratch,
        compiler_params=pltpu.CompilerParams(vmem_limit_bytes=24 * 1024 * 1024),
        cost_estimate=pl.CostEstimate(
            flops=flops, bytes_accessed=4 * sum(a.size for a in args), transcendentals=0
        ),
    )(*args)


def near_pair(t, times):
    return t + 1 - 2 * (t % 2)


def far_pair(t, times):
    return (t - 1 + 2 * (t % 2)) % times


def shards(particles, cell_points, cell_counts, brownian):
    features = particles.shape[1]
    block = particles.reshape(-1, LANES)
    cells = cell_points.reshape(-1, LANES)
    noise = brownian.transpose(1, 0, 2)
    share = brownian.shape[2]
    cell_size, times, blocks = (lax.axis_size(name) for name in ("cell", "tm", "particle"))
    shares = cell_size // 2
    width = cell_points.shape[2]

    def over_cell(x, by):
        return lax.ppermute(x, "cell", [(c, c ^ by) for c in range(cell_size)])

    def over_time(x, pair):
        return lax.ppermute(x, "tm", [(t, pair(t, times)) for t in range(times)])

    def over_particle(x, by):
        return lax.ppermute(x, "particle", [(p, (p + by) % blocks) for p in range(blocks)])

    near_cells = over_cell(cells, 1)
    others = [over_particle(block, by) for by in range(1, blocks)]
    sides = [over_time(block, pair) for pair in (near_pair, far_pair)]

    part = jax.ShapeDtypeStruct((GROUP, share), f32)
    two_parts = jax.ShapeDtypeStruct((2 * GROUP, share), f32)
    operand = jax.ShapeDtypeStruct((6 * GROUP, width), bf16)
    side_operand = jax.ShapeDtypeStruct((6 * GROUP, particles.shape[2]), bf16)
    positions = call(number_cells, jax.ShapeDtypeStruct((8, width), jnp.int32), (), 10**10)
    parts, fit_queries, own_operand = call(
        functools.partial(fit_first, features, share),
        (
            jax.ShapeDtypeStruct((shares - 1, GROUP, share), f32),
            jax.ShapeDtypeStruct(((shares - 1) * share, 6 * GROUP), bf16),
            operand,
        ),
        (cell_counts, positions, block, cells),
        10**9,
        counts=True,
    )
    near_operand, *sent_fits = call(
        functools.partial(fit_second, features, share),
        (operand,) + (part,) * (shares - 1),
        (cell_counts, positions, fit_queries, parts, near_cells),
        10**9,
        counts=True,
    )
    fits = [over_cell(x, 2 * by) for by, x in zip(range(1, shares), sent_fits)]
    side_operands = call(
        functools.partial(bridge_others, features, share, blocks),
        (side_operand, side_operand) + (two_parts,) * (blocks - 1),
        (*sides, *others),
        10**9,
    )
    pulls = [over_particle(x, -by) for by, x in zip(range(1, blocks), side_operands[2:])]
    own_fit, own_pull = call(
        functools.partial(for_own, features, share),
        (part, two_parts),
        (block, own_operand, near_operand, *side_operands[:2]),
        10**9,
    )
    out = jax.ShapeDtypeStruct(noise.shape, f32)
    drift, moved = call(
        functools.partial(finish, features, share, blocks),
        (out, out),
        (block, noise, own_pull, *pulls, own_fit, *fits),
        10**6,
        out_spec=pl.BlockSpec(memory_space=pltpu.HBM),
        scratch=[
            pltpu.VMEM(noise.shape, f32),
            pltpu.VMEM(noise.shape, f32),
            pltpu.SemaphoreType.DMA((2,)),
        ],
    )
    return drift.transpose(1, 0, 2), moved.transpose(1, 0, 2)


def solution(mesh):
    in_specs = (
        P("tm", None, "particle"),
        P("tm", None, "cell"),
        P(),
        P("tm", None, ("particle", "cell")),
    )
    out_specs = (P("tm", None, ("particle", "cell")), P("tm", None, ("particle", "cell")))
    return jax.shard_map(shards, mesh=mesh, in_specs=in_specs, out_specs=out_specs, check_vma=False)
```

time: 23.4 us -> 19.2 us (0.82)
  the two profiles are of different devices: /device:TPU:1 before, /device:TPU:0 now
where the time goes in v2:
time: 19.2 us; the launch traced here: 19.1 us
  starting transfers between devices  9.45 us (49%)
  Pallas kernels  7.99 us (42%)
  waiting for transfers between devices  0.88 us (5%)
  between operations  0.73 us (4%)
    pallas_call x6, Pallas kernels, call(): pl.pallas_call(kernel, out_shape=out_shape, in_specs=[SMEM if counts and...  7.99 us
    ppermute x2, starting transfers between devices, over_cell(): return lax.ppermute(x, 'cell', [(c, c ^ by) for c in range(cell_size)])  4.71 us
    ppermute x2, starting transfers between devices, over_particle(): lax.ppermute(x, 'particle', [(p, (p + by) % blocks) for p in range(blocks)])  3.13 us
    ppermute x2, starting transfers between devices, over_time(): return lax.ppermute(x, 'tm', [(t, pair(t, times)) for t in range(times)])  1.61 us
    ppermute x2, waiting for transfers between devices, over_time(): return lax.ppermute(x, 'tm', [(t, pair(t, times)) for t in range(times)])  0.87 us
  transfers between devices with their start and end apart: 6, of which 1 were waited for; matrix products, arithmetic and copies ran while one was open for 0% of the time, Pallas kernels for 38%

profile of v2, /device:TPU:0, one launch (start us, length us, event | category | flops | bytes accessed | tf_op | source)
XLA Modules:
  0.0 19.1 jit_solution(14379563491294144469)
XLA Ops:
  0.6 3.1 %collective-permute-start.3 = (f32[240,128]{1,0:T(8,128)}, f32[240,128]{1,0:T(8,128)S(1)}, u32[]{:S(2)}, u32[]{:S(2)}) collective-permute-start(f32[240,128]{1,0:T(8,128)} %bitcast.5), channel_id=1, source_target_pairs={{0,4},{4,0},{1,5},{5,1},{2,6},{6,2},{3,7},{7,3},{8,12},{12,8},{9,1... | collective-permute-start | bytes 368648 | tf_op jit(solution)/shard_map/ppermute | solution.py:266
  3.7 0.7 %collective-permute-start.2 = (f32[240,128]{1,0:T(8,128)}, f32[240,128]{1,0:T(8,128)S(1)}, u32[]{:S(2)}, u32[]{:S(2)}) collective-permute-start(f32[240,128]{1,0:T(8,128)} %bitcast.6), channel_id=1, source_target_pairs={{0,24},{8,16},{16,8},{24,0},{1,25},{9,17},{17,9},{25,1},{2,26},{10... | collective-permute-start | bytes 368648 | tf_op jit(solution)/shard_map/ppermute | solution.py:263
  4.3 1.0 %collective-permute-start.1 = (f32[240,128]{1,0:T(8,128)}, f32[240,128]{1,0:T(8,128)S(1)}, u32[]{:S(2)}, u32[]{:S(2)}) collective-permute-start(f32[240,128]{1,0:T(8,128)} %bitcast.7), channel_id=1, source_target_pairs={{0,8},{8,0},{16,24},{24,16},{1,9},{9,1},{17,25},{25,17},{2,10},{10... | collective-permute-start | bytes 368648 | tf_op jit(solution)/shard_map/ppermute | solution.py:263
  5.3 0.0 copy-start
  5.3 0.0 copy-start.2
  5.3 0.0 copy-start.3
  5.3 1.6 %collective-permute-start = (f32[240,128]{1,0:T(8,128)}, f32[240,128]{1,0:T(8,128)S(1)}, u32[]{:S(2)}, u32[]{:S(2)}) collective-permute-start(f32[240,128]{1,0:T(8,128)} %bitcast.12), channel_id=1, source_target_pairs={{0,1},{1,0},{2,3},{3,2},{4,5},{5,4},{6,7},{7,6},{8,9},{9,8},{10,11... | collective-permute-start | bytes 368648 | tf_op jit(solution)/shard_map/ppermute | solution.py:260
  6.9 0.0 copy-done
  6.9 0.0 copy-done.2
  6.9 0.0 copy-done.3
  6.9 1.7 %shard_map.60 = (f32[1,32,256]{2,1,0:T(8,128)S(1)}, bf16[256,192]{1,0:T(8,128)(2,1)S(1)}, bf16[192,1024]{1,0:T(8,128)(2,1)S(1)}) custom-call(s32[4]{0:T(128)S(1)} %copy-done.3, s32[8,1024]{1,0:T(8,128)S(1)} %shard_map.59.positions_ref, f32[240,128]{1,0:T(8,128)S(1)} %bitcast.8, f32[240,128]{1,0:T(8,128)S(1)} %bitcast.13), custom_call_target="tpu_custom_call" | custom-call | flops 1000000000 | bytes 278544 | tf_op jit(solution)/shard_map/pallas_call | solution.py:228
  8.6 0.0 collective-permute-done.3.refs_2_
  8.6 0.9 %collective-permute-done.2.refs_1_ = f32[240,128]{1,0:T(8,128)S(1)} collective-permute-done((f32[240,128]{1,0:T(8,128)}, f32[240,128]{1,0:T(8,128)S(1)}, u32[]{:S(2)}, u32[]{:S(2)}) %collective-permute-start.2) | collective-permute-done | bytes 122912 | tf_op jit(solution)/shard_map/ppermute | solution.py:263
  9.4 0.0 collective-permute-done.1.refs_0_
  9.4 1.4 %shard_map.62 = (bf16[192,1024]{1,0:T(8,128)(2,1)S(1)}, bf16[192,1024]{1,0:T(8,128)(2,1)S(1)}, f32[64,256]{1,0:T(8,128)S(1)}) custom-call(f32[240,128]{1,0:T(8,128)S(1)} %collective-permute-done.1.refs_0_, f32[240,128]{1,0:T(8,128)S(1)} %collective-permute-done.2.refs_1_, f32[240,128]{1,0:T(8,128)S(1)} %collective-permute-done.3.refs_2_), custom_call_target="tpu_custom_call" | custom-call | flops 1000000000 | bytes 368640 | tf_op jit(solution)/shard_map/pallas_call | solution.py:228
  10.9 0.1 collective-permute-start.4
  11.0 0.0 collective-permute-done.refs_0_
  11.0 1.7 %shard_map.61 = (bf16[192,1024]{1,0:T(8,128)(2,1)S(1)}, f32[32,256]{1,0:T(8,128)S(1)}) custom-call(s32[4]{0:T(128)S(1)} %copy-done.3, s32[8,1024]{1,0:T(8,128)S(1)} %shard_map.59.positions_ref, bf16[256,192]{1,0:T(8,128)(2,1)S(1)} %get-tuple-element.15.queries_ref, f32[1,32,256]{2,1,0:T(8,128)S(1)} %get-tuple-element.16.parts_ref, ...), custom_call_target="tpu_custom_call" | custom-call | flops 1000000000 | bytes 385040 | tf_op jit(solution)/shard_map/pallas_call | solution.py:228
  12.6 3.1 %collective-permute-start.5 = (f32[32,256]{1,0:T(8,128)S(1)}, f32[32,256]{1,0:T(8,128)S(1)}, u32[]{:S(2)}, u32[]{:S(2)}) collective-permute-start(f32[32,256]{1,0:T(8,128)S(1)} %get-tuple-element.23), channel_id=1, source_target_pairs={{0,2},{1,3},{2,0},{3,1},{4,6},{5,7},{6,4},{7,5},{8,10},{9,11},{10,... | collective-permute-start | bytes 98312 | tf_op jit(solution)/shard_map/ppermute | solution.py:260
  15.8 2.5 %shard_map.63 = (f32[32,256]{1,0:T(8,128)S(1)}, f32[64,256]{1,0:T(8,128)S(1)}) custom-call(f32[240,128]{1,0:T(8,128)S(1)} %bitcast.9, bf16[192,1024]{1,0:T(8,128)(2,1)S(1)} %get-tuple-element.14.refs_0_, bf16[192,1024]{1,0:T(8,128)(2,1)S(1)} %get-tuple-element.17.refs_1_, bf16[192,1024]{1,0:T(8,128)(2,1)S(1)} %get-tuple-element.18.refs_2_, ...), custom_call_target="tpu_custom_call" | custom-call | flops 1000000000 | bytes 3268608 | tf_op jit(solution)/shard_map/pallas_call | solution.py:228
  18.3 0.0 collective-permute-done.5.refs_3_
  18.3 0.0 collective-permute-done.4.refs_1_
  18.3 0.0 copy-done.1
  18.3 0.7 %shard_map.64 = (f32[30,1,256]{2,1,0:T(1,128)}, f32[30,1,256]{2,1,0:T(1,128)}) custom-call(f32[240,128]{1,0:T(8,128)S(1)} %bitcast.10, f32[30,1,256]{2,1,0:T(1,128)S(1)} %bitcast.11, f32[64,256]{1,0:T(8,128)S(1)} %get-tuple-element.20.refs_0_, f32[64,256]{1,0:T(8,128)S(1)} %collective-permute-done.4.refs_1_, f32[32,256]{1,0:T(8,128)S(1)} %get-tuple-element.22.refs_2_, ...), custom_call_target="tpu_custom_call" | custom-call | flops 1000000 | bytes 350208 | tf_op jit(solution)/shard_map/pallas_call | solution.py:228
  (2 shorter events, 0.0 us)
Async XLA Ops:
  0.6 7.9 %collective-permute-start.3 = (f32[240,128]{1,0:T(8,128)}, f32[240,128]{1,0:T(8,128)S(1)}, u32[]{:S(2)}, u32[]{:S(2)}) collective-permute-start(f32[240,128]{1,0:T(8,128)} %bitcast.5), channel_id=1, source_target_pairs={{0,4},{4,0},{1,5},{5,1},{2,6},{6,2},{3,7},{7,3},{8,12},{12,8},{9,1... | collective-permute-start | bytes 368648 | tf_op jit(solution)/shard_map/ppermute | solution.py:266
  3.7 5.8 %collective-permute-start.2 = (f32[240,128]{1,0:T(8,128)}, f32[240,128]{1,0:T(8,128)S(1)}, u32[]{:S(2)}, u32[]{:S(2)}) collective-permute-start(f32[240,128]{1,0:T(8,128)} %bitcast.6), channel_id=1, source_target_pairs={{0,24},{8,16},{16,8},{24,0},{1,25},{9,17},{17,9},{25,1},{2,26},{10... | collective-permute-start | bytes 368648 | tf_op jit(solution)/shard_map/ppermute | solution.py:263
  4.3 5.1 %collective-permute-start.1 = (f32[240,128]{1,0:T(8,128)}, f32[240,128]{1,0:T(8,128)S(1)}, u32[]{:S(2)}, u32[]{:S(2)}) collective-permute-start(f32[240,128]{1,0:T(8,128)} %bitcast.7), channel_id=1, source_target_pairs={{0,8},{8,0},{16,24},{24,16},{1,9},{9,1},{17,25},{25,17},{2,10},{10... | collective-permute-start | bytes 368648 | tf_op jit(solution)/shard_map/ppermute | solution.py:263
  5.3 1.6 %copy-start = (f32[1,30,1024]{2,0,1:T(1,128)S(1)}, f32[1,30,1024]{2,0,1:T(1,128)}, u32[]{:S(2)}) copy-start(f32[1,30,1024]{2,0,1:T(1,128)} %param.4) | copy-start | bytes 368644
  5.3 1.6 %copy-start.2 = (f32[1,30,1024]{2,0,1:T(1,128)S(1)}, f32[1,30,1024]{2,0,1:T(1,128)}, u32[]{:S(2)}) copy-start(f32[1,30,1024]{2,0,1:T(1,128)} %param.5) | copy-start | bytes 368644
  5.3 1.6 %copy-start.3 = (s32[4]{0:T(128)S(1)}, s32[4]{0:T(128)}, u32[]{:S(2)}) copy-start(s32[4]{0:T(128)} %counts_ref.3) | copy-start | bytes 52
  5.3 5.7 %collective-permute-start = (f32[240,128]{1,0:T(8,128)}, f32[240,128]{1,0:T(8,128)S(1)}, u32[]{:S(2)}, u32[]{:S(2)}) collective-permute-start(f32[240,128]{1,0:T(8,128)} %bitcast.12), channel_id=1, source_target_pairs={{0,1},{1,0},{2,3},{3,2},{4,5},{5,4},{6,7},{7,6},{8,9},{9,8},{10,11... | collective-permute-start | bytes 368648 | tf_op jit(solution)/shard_map/ppermute | solution.py:260
  10.9 7.4 %collective-permute-start.4 = (f32[64,256]{1,0:T(8,128)S(1)}, f32[64,256]{1,0:T(8,128)S(1)}, u32[]{:S(2)}, u32[]{:S(2)}) collective-permute-start(f32[64,256]{1,0:T(8,128)S(1)} %get-tuple-element.21), channel_id=1, source_target_pairs={{0,4},{4,0},{1,5},{5,1},{2,6},{6,2},{3,7},{7,3},{8,12},{12,8},{9,1... | collective-permute-start | bytes 196616 | tf_op jit(solution)/shard_map/ppermute | solution.py:266
  12.6 5.7 %collective-permute-start.5 = (f32[32,256]{1,0:T(8,128)S(1)}, f32[32,256]{1,0:T(8,128)S(1)}, u32[]{:S(2)}, u32[]{:S(2)}) collective-permute-start(f32[32,256]{1,0:T(8,128)S(1)} %get-tuple-element.23), channel_id=1, source_target_pairs={{0,2},{1,3},{2,0},{3,1},{4,6},{5,7},{6,4},{7,5},{8,10},{9,11},{10,... | collective-permute-start | bytes 98312 | tf_op jit(solution)/shard_map/ppermute | solution.py:260
  15.8 2.6 %copy-start.1 = (f32[1,30,256]{2,0,1:T(1,128)S(1)}, f32[1,30,256]{2,0,1:T(1,128)}, u32[]{:S(2)}) copy-start(f32[1,30,256]{2,0,1:T(1,128)} %param.7) | copy-start | bytes 92164

commit v3 on v2

--- a/solution.py
+++ b/solution.py
@@ -7,6 +7,7 @@
 from jax.experimental import pallas as pl
 from jax.experimental.pallas import tpu as pltpu
 from jax.sharding import PartitionSpec as P
+
 
 DATA_VAR = 2.0
 BRIDGE_VAR = 1.5
@@ -110,7 +111,9 @@
 
 
 def usable_cells(counts_ref, positions_ref, which):
-    count = counts_ref[lax.axis_index("tm")]
+    counts = counts_ref[...].astype(f32)
+    here = lax.broadcasted_iota(jnp.int32, counts.shape, 1) == lax.axis_index("tm")
+    count = jnp.sum(jnp.where(here, counts, 0.0), 1, keepdims=True).astype(jnp.int32)
     return positions_ref[0:1, :] + which * positions_ref.shape[1] < count
 
 
@@ -132,16 +135,15 @@
 
 
 def fit_first(features, share, counts_ref, positions_ref, block_ref, cells_ref, *refs):
-    parts_ref, queries_ref, operand_ref = refs
+    parts_ref, queries_ref = refs
     columns = [
-        share_columns(block_ref, features, lax.bitwise_xor(own_cell(), 2 * (j + 1)), share)
+        share_columns(block_ref, features, lax.bitwise_xor(own_cell(), 2 * j), share)
         for j in range(parts_ref.shape[0])
     ]
     queries = query_operand(jnp.concatenate(columns, 1), FIT_SCALE)
     queries_ref[...] = queries
     usable = usable_cells(counts_ref, positions_ref, own_cell())
     targets = target_operand(whole(cells_ref, features), FIT_SCALE, usable)
-    operand_ref[...] = targets
     parts = partial_sums(queries, targets)
     for j in range(parts_ref.shape[0]):
         parts_ref[j] = parts[:, j * share : (j + 1) * share]
@@ -152,56 +154,46 @@
     usable = usable_cells(counts_ref, positions_ref, lax.bitwise_xor(own_cell(), 1))
     targets = target_operand(whole(cells_ref, features), FIT_SCALE, usable)
     operand_ref[...] = targets
-    parts = partial_sums(queries_ref[...], targets)
+    parts = partial_sums(queries_ref[share:, :], targets)
     for j, fit_ref in enumerate(fit_refs):
-        fit_ref[...] = merged([parts_ref[j], parts[:, j * share : (j + 1) * share]])
-
-
-def bridge_others(features, share, blocks, *refs):
-    side_refs, other_refs = refs[:2], refs[2 : 1 + blocks]
-    operand_refs, pull_refs = refs[1 + blocks : 3 + blocks], refs[3 + blocks :]
-    queries = query_operand(
-        jnp.concatenate([share_columns(r, features, own_cell(), share) for r in other_refs], 1),
-        BRIDGE_SCALE,
-    )
-    for side, (side_ref, operand_ref) in enumerate(zip(side_refs, operand_refs)):
-        targets = target_operand(whole(side_ref, features), BRIDGE_SCALE)
-        operand_ref[...] = targets
-        parts = partial_sums(queries, targets)
-        for j, pull_ref in enumerate(pull_refs):
-            pull_ref[side * GROUP : (side + 1) * GROUP, :] = parts[:, j * share : (j + 1) * share]
-
-
-def for_own(features, share, block_ref, *refs):
-    own_ref, near_ref, *side_refs = refs[:4]
-    fit_ref, pull_ref = refs[4:]
-    x = share_columns(block_ref, features, own_cell(), share)
-    queries = query_operand(x, FIT_SCALE)
-    fit_ref[...] = merged([partial_sums(queries, ref[...]) for ref in (own_ref, near_ref)])
-    queries = query_operand(x, BRIDGE_SCALE)
-    for side, side_ref in enumerate(side_refs):
-        pull_ref[side * GROUP : (side + 1) * GROUP, :] = partial_sums(queries, side_ref[...])
-
-
-def finish(features, share, blocks, block_ref, noise_ref, *refs):
-    pull_refs, fit_refs = refs[:blocks], refs[blocks:-5]
+        fit_ref[...] = merged([parts_ref[j + 1], parts[:, j * share : (j + 1) * share]])
+
+
+def bridge(queries, key_refs, features):
+    targets = [target_operand(whole(ref, features), BRIDGE_SCALE) for ref in key_refs]
+    return merged([partial_sums(queries, target) for target in targets])
+
+
+def own_near(features, share, block_ref, fit_queries_ref, parts_ref, operand_ref, *refs):
+    *key_refs, fit_ref, pull_ref, queries_ref = refs
+    fit_ref[...] = merged([parts_ref[0], partial_sums(fit_queries_ref[:share, :], operand_ref[...])])
+    queries = query_operand(share_columns(block_ref, features, own_cell(), share), BRIDGE_SCALE)
+    queries_ref[...] = queries
+    pull_ref[...] = bridge(queries, key_refs, features)
+
+
+def own_far(features, queries_ref, *refs):
+    *key_refs, pull_ref = refs
+    pull_ref[...] = bridge(queries_ref[...], key_refs, features)
+
+
+def finish(features, share, block_ref, noise_ref, near_ref, far_ref, *refs):
+    fit_refs = refs[:-5]
     drift_out, moved_out, drift_ref, moved_ref, sem = refs[-5:]
     per_share = share // LANES
     first = own_cell() * per_share
     time, times = lax.axis_index("tm"), lax.axis_size("tm")
     step = 1 - 2 * lax.rem(time, 2)
     fit_mean = mean_of(merged([ref[...] for ref in fit_refs]))
-    side_means = [
-        mean_of(merged([ref[side * GROUP : (side + 1) * GROUP, :] for ref in pull_refs]))
-        for side in range(2)
+    sides = [
+        (mean_of(ref[...]), jnp.logical_and(other >= 0, other < times))
+        for ref, other in ((near_ref, time + step), (far_ref, time - step))
     ]
-    partners = [time + step, time - step]
-    there = [jnp.logical_and(other >= 0, other < times) for other in partners]
     for k in range(per_share):
         lanes = slice(k * LANES, (k + 1) * LANES)
         x = block_ref[pl.ds(first + k, features, stride=block_ref.shape[0] // features), :]
         gradient = (x - fit_mean[:features, lanes]) / DATA_VAR
-        for mean, present in zip(side_means, there):
+        for mean, present in sides:
             gradient = gradient + jnp.where(present, (x - mean[:features, lanes]) / BRIDGE_VAR, 0.0)
         drift = -gradient
         drift_ref[:, 0, lanes] = drift
@@ -221,14 +213,13 @@
 
 
 VMEM = pl.BlockSpec(memory_space=pltpu.VMEM)
-SMEM = pl.BlockSpec(memory_space=pltpu.SMEM)
-
-
-def call(kernel, out_shape, args, flops, counts=False, out_spec=VMEM, scratch=()):
+
+
+def call(kernel, out_shape, args, flops, out_spec=VMEM, scratch=()):
     return pl.pallas_call(
         kernel,
         out_shape=out_shape,
-        in_specs=[SMEM if counts and k == 0 else VMEM for k in range(len(args))],
+        in_specs=[VMEM] * len(args),
         out_specs=jax.tree.map(lambda _: out_spec, out_shape),
         scratch_shapes=scratch,
         compiler_params=pltpu.CompilerParams(vmem_limit_bytes=24 * 1024 * 1024),
@@ -259,58 +250,55 @@
     def over_cell(x, by):
         return lax.ppermute(x, "cell", [(c, c ^ by) for c in range(cell_size)])
 
-    def over_time(x, pair):
-        return lax.ppermute(x, "tm", [(t, pair(t, times)) for t in range(times)])
-
-    def over_particle(x, by):
-        return lax.ppermute(x, "particle", [(p, (p + by) % blocks) for p in range(blocks)])
+    def over_time(pair, by):
+        places = [(t, p) for t in range(times) for p in range(blocks)]
+        return lax.ppermute(
+            block,
+            ("tm", "particle"),
+            [(t * blocks + p, pair(t, times) * blocks + (p + by) % blocks) for t, p in places],
+        )
 
     near_cells = over_cell(cells, 1)
-    others = [over_particle(block, by) for by in range(1, blocks)]
-    sides = [over_time(block, pair) for pair in (near_pair, far_pair)]
+    keys = {}
+    for side, pair in (("near", near_pair), ("far", far_pair)):
+        keys[side] = [over_time(pair, 0)]
+        keys[side] += [over_time(pair, by) for by in range(1, blocks)]
 
     part = jax.ShapeDtypeStruct((GROUP, share), f32)
-    two_parts = jax.ShapeDtypeStruct((2 * GROUP, share), f32)
     operand = jax.ShapeDtypeStruct((6 * GROUP, width), bf16)
-    side_operand = jax.ShapeDtypeStruct((6 * GROUP, particles.shape[2]), bf16)
+    own_queries = jax.ShapeDtypeStruct((share, 6 * GROUP), bf16)
     positions = call(number_cells, jax.ShapeDtypeStruct((8, width), jnp.int32), (), 10**10)
-    parts, fit_queries, own_operand = call(
+    counts = cell_counts[None]
+    parts, fit_queries = call(
         functools.partial(fit_first, features, share),
         (
-            jax.ShapeDtypeStruct((shares - 1, GROUP, share), f32),
-            jax.ShapeDtypeStruct(((shares - 1) * share, 6 * GROUP), bf16),
-            operand,
+            jax.ShapeDtypeStruct((shares, GROUP, share), f32),
+            jax.ShapeDtypeStruct((shares * share, 6 * GROUP), bf16),
         ),
-        (cell_counts, positions, block, cells),
+        (counts, positions, block, cells),
         10**9,
-        counts=True,
     )
     near_operand, *sent_fits = call(
         functools.partial(fit_second, features, share),
         (operand,) + (part,) * (shares - 1),
-        (cell_counts, positions, fit_queries, parts, near_cells),
+        (counts, positions, fit_queries, parts, near_cells),
         10**9,
-        counts=True,
     )
     fits = [over_cell(x, 2 * by) for by, x in zip(range(1, shares), sent_fits)]
-    side_operands = call(
-        functools.partial(bridge_others, features, share, blocks),
-        (side_operand, side_operand) + (two_parts,) * (blocks - 1),
-        (*sides, *others),
+    own_fit, near_pull, bridge_queries = call(
+        functools.partial(own_near, features, share),
+        (part, part, own_queries),
+        (block, fit_queries, parts, near_operand, *keys["near"]),
         10**9,
     )
-    pulls = [over_particle(x, -by) for by, x in zip(range(1, blocks), side_operands[2:])]
-    own_fit, own_pull = call(
-        functools.partial(for_own, features, share),
-        (part, two_parts),
-        (block, own_operand, near_operand, *side_operands[:2]),
-        10**9,
+    far_pull = call(
+        functools.partial(own_far, features), part, (bridge_queries, *keys["far"]), 10**9
     )
     out = jax.ShapeDtypeStruct(noise.shape, f32)
     drift, moved = call(
-        functools.partial(finish, features, share, blocks),
+        functools.partial(finish, features, share),
         (out, out),
-        (block, noise, own_pull, *pulls, own_fit, *fits),
+        (block, noise, near_pull, far_pull, own_fit, *fits),
         10**6,
         out_spec=pl.BlockSpec(memory_space=pltpu.HBM),
         scratch=[

time: 19.2 us -> 19.4 us (1.010)
  Pallas kernels: 7.99 us -> 7.34 us
  local copies, waits for them, and re-layouts: 0.01 us -> 0.65 us
  waiting for transfers between devices: 0.88 us -> 1.34 us
  starting transfers between devices: 9.45 us -> 9.23 us
    ppermute x2, waiting for transfers between devices: 0.01 us -> 1.33 us  [over_cell(): return lax.ppermute(x, 'cell', [(c, c ^ by) for c in range(cell_size)])]
    ppermute x4, waiting for transfers between devices: 0.87 us -> 0.01 us  [over_time(): lax.ppermute(block, ('tm', 'particle'), [(t * blocks + p, pair(t, times)...]
    pallas_call x6, Pallas kernels: 7.99 us -> 7.34 us  [call(): pl.pallas_call(kernel, out_shape=out_shape, in_specs=[VMEM] * len(args),...]
    unnamed x8, local copies, waits for them, and re-layouts: 0.01 us -> 0.65 us
    ppermute x4, starting transfers between devices: 4.74 us -> 4.4 us  [over_time(): lax.ppermute(block, ('tm', 'particle'), [(t * blocks + p, pair(t, times)...]
  transfers between devices with their start and end apart: 6 -> 6, of which waited for: 1 -> 1; matrix products, arithmetic and copies ran while one was open for 0% -> 0% of each run, Pallas kernels for 38% -> 34%
where the time goes in v3:
time: 19.4 us; the launch traced here: 19.3 us
  starting transfers between devices  9.23 us (48%)
  Pallas kernels  7.34 us (38%)
  waiting for transfers between devices  1.34 us (7%)
  between operations  0.72 us (4%)
  local copies, waits for them, and re-layouts  0.65 us (3%)
    pallas_call x6, Pallas kernels, call(): pl.pallas_call(kernel, out_shape=out_shape, in_specs=[VMEM] * len(args),...  7.34 us
    ppermute x2, starting transfers between devices, over_cell(): return lax.ppermute(x, 'cell', [(c, c ^ by) for c in range(cell_size)])  4.83 us
    ppermute x4, starting transfers between devices, over_time(): lax.ppermute(block, ('tm', 'particle'), [(t * blocks + p, pair(t, times)...  4.4 us
    ppermute x2, waiting for transfers between devices, over_cell(): return lax.ppermute(x, 'cell', [(c, c ^ by) for c in range(cell_size)])  1.33 us
    unnamed x8, local copies, waits for them, and re-layouts  0.65 us
  transfers between devices with their start and end apart: 6, of which 1 were waited for; matrix products, arithmetic and copies ran while one was open for 0% of the time, Pallas kernels for 34%

profile of v3, /device:TPU:0, one launch (start us, length us, event | category | flops | bytes accessed | tf_op | source)
XLA Modules:
  0.0 19.3 jit_solution(13077005466620689280)
XLA Ops:
  0.6 0.6 %collective-permute-start.1 = (f32[240,128]{1,0:T(8,128)}, f32[240,128]{1,0:T(8,128)S(1)}, u32[]{:S(2)}, u32[]{:S(2)}) collective-permute-start(f32[240,128]{1,0:T(8,128)} %bitcast.6), channel_id=1, source_target_pairs={{0,8},{4,12},{8,0},{12,4},{16,24},{20,28},{24,16},{28,20},{1,9},{5... | collective-permute-start | bytes 368648 | tf_op jit(solution)/shard_map/ppermute | solution.py:255
  1.2 2.6 %collective-permute-start.2 = (f32[240,128]{1,0:T(8,128)}, f32[240,128]{1,0:T(8,128)S(1)}, u32[]{:S(2)}, u32[]{:S(2)}) collective-permute-start(f32[240,128]{1,0:T(8,128)} %bitcast.7), channel_id=1, source_target_pairs={{0,12},{4,8},{8,4},{12,0},{16,28},{20,24},{24,20},{28,16},{1,13},{... | collective-permute-start | bytes 368648 | tf_op jit(solution)/shard_map/ppermute | solution.py:255
  3.8 1.2 %collective-permute-start.3 = (f32[240,128]{1,0:T(8,128)}, f32[240,128]{1,0:T(8,128)S(1)}, u32[]{:S(2)}, u32[]{:S(2)}) collective-permute-start(f32[240,128]{1,0:T(8,128)} %bitcast.8), channel_id=1, source_target_pairs={{0,24},{4,28},{8,16},{12,20},{16,8},{20,12},{24,0},{28,4},{1,25},{... | collective-permute-start | bytes 368648 | tf_op jit(solution)/shard_map/ppermute | solution.py:255
  5.0 0.0 collective-permute-start.4
  5.0 0.0 copy-start
  5.0 0.0 copy-start.2
  5.0 2.0 %collective-permute-start = (f32[240,128]{1,0:T(8,128)}, f32[240,128]{1,0:T(8,128)S(1)}, u32[]{:S(2)}, u32[]{:S(2)}) collective-permute-start(f32[240,128]{1,0:T(8,128)} %bitcast.14), channel_id=1, source_target_pairs={{0,1},{1,0},{2,3},{3,2},{4,5},{5,4},{6,7},{7,6},{8,9},{9,8},{10,11... | collective-permute-start | bytes 368648 | tf_op jit(solution)/shard_map/ppermute | solution.py:251
  7.1 0.0 copy-done
  7.1 0.0 copy-done.2
  7.1 0.6 %copy-done.3 = s32[4]{0:T(128)S(1)} copy-done((s32[4]{0:T(128)S(1)}, s32[4]{0:T(128)}, u32[]{:S(2)}) %copy-start.3) | copy-done | bytes 40
  7.7 1.8 %shard_map.60 = (f32[2,32,256]{2,1,0:T(8,128)S(1)}, bf16[512,192]{1,0:T(8,128)(2,1)S(1)}) custom-call(s32[1,4]{1,0:T(1,128)S(1)} %bitcast.16, s32[8,1024]{1,0:T(8,128)S(1)} %shard_map.59.positions_ref, f32[240,128]{1,0:T(8,128)S(1)} %bitcast.10, f32[240,128]{1,0:T(8,128)S(1)} %bitcast.15), custom_call_target="tpu_custom_call" | custom-call | flops 1000000000 | bytes 278544 | tf_op jit(solution)/shard_map/pallas_call | solution.py:219
  9.6 1.3 %collective-permute-done.refs_0_ = f32[240,128]{1,0:T(8,128)S(1)} collective-permute-done((f32[240,128]{1,0:T(8,128)}, f32[240,128]{1,0:T(8,128)S(1)}, u32[]{:S(2)}, u32[]{:S(2)}) %collective-permute-start) | collective-permute-done | bytes 122912 | tf_op jit(solution)/shard_map/ppermute | solution.py:251
  10.9 1.2 %shard_map.61 = (bf16[192,1024]{1,0:T(8,128)(2,1)S(1)}, f32[32,256]{1,0:T(8,128)S(1)}) custom-call(s32[1,4]{1,0:T(1,128)S(1)} %bitcast.17, s32[8,1024]{1,0:T(8,128)S(1)} %shard_map.59.positions_ref, bf16[512,192]{1,0:T(8,128)(2,1)S(1)} %get-tuple-element.11.queries_ref.fit_queries_ref, f32[2,32,256]{2,1,0:T(8,128)S(1)} %get-tuple-element.12.parts_ref, ...), custom_call_target="tpu_custom_call" | custom-call | flops 1000000000 | bytes 614416 | tf_op jit(solution)/shard_map/pallas_call | solution.py:219
  12.0 2.8 %collective-permute-start.5 = (f32[32,256]{1,0:T(8,128)S(1)}, f32[32,256]{1,0:T(8,128)S(1)}, u32[]{:S(2)}, u32[]{:S(2)}) collective-permute-start(f32[32,256]{1,0:T(8,128)S(1)} %get-tuple-element.17), channel_id=1, source_target_pairs={{0,2},{1,3},{2,0},{3,1},{4,6},{5,7},{6,4},{7,5},{8,10},{9,11},{10,... | collective-permute-start | bytes 98312 | tf_op jit(solution)/shard_map/ppermute | solution.py:251
  14.8 0.0 collective-permute-done.1.refs_0_
  14.8 0.0 collective-permute-done.2.refs_1_
  14.8 2.2 %shard_map.62 = (f32[32,256]{1,0:T(8,128)S(1)}, f32[32,256]{1,0:T(8,128)S(1)}, bf16[256,192]{1,0:T(8,128)(2,1)S(1)}) custom-call(f32[240,128]{1,0:T(8,128)S(1)} %bitcast.11, bf16[512,192]{1,0:T(8,128)(2,1)S(1)} %get-tuple-element.11.queries_ref.fit_queries_ref, f32[2,32,256]{2,1,0:T(8,128)S(1)} %get-tuple-element.12.parts_ref, ...), custom_call_target="tpu_custom_call" | custom-call | flops 1000000000 | bytes 1613824 | tf_op jit(solution)/shard_map/pallas_call | solution.py:219
  17.1 0.0 collective-permute-done.3.refs_0_
  17.1 0.0 collective-permute-done.4.refs_1_
  17.1 0.0 copy-start.1
  17.1 1.4 %shard_map.63.far_ref = f32[32,256]{1,0:T(8,128)S(1)} custom-call(bf16[256,192]{1,0:T(8,128)(2,1)S(1)} %get-tuple-element.15.queries_ref, f32[240,128]{1,0:T(8,128)S(1)} %collective-permute-done.3.refs_0_, f32[240,128]{1,0:T(8,128)S(1)} %collective-permute-done.4.refs_1_), custom_call_target="tpu_custom_call" | custom-call | flops 1000000000 | bytes 442368 | tf_op jit(solution)/shard_map/pallas_call | solution.py:219
  18.5 0.0 collective-permute-done.5.refs_1_
  18.5 0.0 copy-done.1
  18.6 0.7 %shard_map.64 = (f32[30,1,256]{2,1,0:T(1,128)}, f32[30,1,256]{2,1,0:T(1,128)}) custom-call(f32[240,128]{1,0:T(8,128)S(1)} %bitcast.12, f32[30,1,256]{2,1,0:T(1,128)S(1)} %bitcast.13, f32[32,256]{1,0:T(8,128)S(1)} %get-tuple-element.14.near_ref, f32[32,256]{1,0:T(8,128)S(1)} %shard_map.63.far_ref, f32[32,256]{1,0:T(8,128)S(1)} %get-tuple-element.16.refs_0_, ...), custom_call_target="tpu_custom_call" | custom-call | flops 1000000 | bytes 284672 | tf_op jit(solution)/shard_map/pallas_call | solution.py:219
  (2 shorter events, 0.0 us)
Async XLA Ops:
  0.6 14.2 %collective-permute-start.1 = (f32[240,128]{1,0:T(8,128)}, f32[240,128]{1,0:T(8,128)S(1)}, u32[]{:S(2)}, u32[]{:S(2)}) collective-permute-start(f32[240,128]{1,0:T(8,128)} %bitcast.6), channel_id=1, source_target_pairs={{0,8},{4,12},{8,0},{12,4},{16,24},{20,28},{24,16},{28,20},{1,9},{5... | collective-permute-start | bytes 368648 | tf_op jit(solution)/shard_map/ppermute | solution.py:255
  1.2 13.7 %collective-permute-start.2 = (f32[240,128]{1,0:T(8,128)}, f32[240,128]{1,0:T(8,128)S(1)}, u32[]{:S(2)}, u32[]{:S(2)}) collective-permute-start(f32[240,128]{1,0:T(8,128)} %bitcast.7), channel_id=1, source_target_pairs={{0,12},{4,8},{8,4},{12,0},{16,28},{20,24},{24,20},{28,16},{1,13},{... | collective-permute-start | bytes 368648 | tf_op jit(solution)/shard_map/ppermute | solution.py:255
  3.8 13.3 %collective-permute-start.3 = (f32[240,128]{1,0:T(8,128)}, f32[240,128]{1,0:T(8,128)S(1)}, u32[]{:S(2)}, u32[]{:S(2)}) collective-permute-start(f32[240,128]{1,0:T(8,128)} %bitcast.8), channel_id=1, source_target_pairs={{0,24},{4,28},{8,16},{12,20},{16,8},{20,12},{24,0},{28,4},{1,25},{... | collective-permute-start | bytes 368648 | tf_op jit(solution)/shard_map/ppermute | solution.py:255
  5.0 12.1 %collective-permute-start.4 = (f32[240,128]{1,0:T(8,128)}, f32[240,128]{1,0:T(8,128)S(1)}, u32[]{:S(2)}, u32[]{:S(2)}) collective-permute-start(f32[240,128]{1,0:T(8,128)} %bitcast.9), channel_id=1, source_target_pairs={{0,28},{4,24},{8,20},{12,16},{16,12},{20,8},{24,4},{28,0},{1,29},{... | collective-permute-start | bytes 368648 | tf_op jit(solution)/shard_map/ppermute | solution.py:255
  5.0 2.1 %copy-start = (f32[1,30,1024]{2,0,1:T(1,128)S(1)}, f32[1,30,1024]{2,0,1:T(1,128)}, u32[]{:S(2)}) copy-start(f32[1,30,1024]{2,0,1:T(1,128)} %param.4) | copy-start | bytes 368644
  5.0 2.1 %copy-start.2 = (f32[1,30,1024]{2,0,1:T(1,128)S(1)}, f32[1,30,1024]{2,0,1:T(1,128)}, u32[]{:S(2)}) copy-start(f32[1,30,1024]{2,0,1:T(1,128)} %param.5) | copy-start | bytes 368644
  5.0 5.8 %collective-permute-start = (f32[240,128]{1,0:T(8,128)}, f32[240,128]{1,0:T(8,128)S(1)}, u32[]{:S(2)}, u32[]{:S(2)}) collective-permute-start(f32[240,128]{1,0:T(8,128)} %bitcast.14), channel_id=1, source_target_pairs={{0,1},{1,0},{2,3},{3,2},{4,5},{5,4},{6,7},{7,6},{8,9},{9,8},{10,11... | collective-permute-start | bytes 368648 | tf_op jit(solution)/shard_map/ppermute | solution.py:251
  7.1 0.7 %copy-start.3 = (s32[4]{0:T(128)S(1)}, s32[4]{0:T(128)}, u32[]{:S(2)}) copy-start(s32[4]{0:T(128)} %param.6) | copy-start | bytes 52
  12.0 6.5 %collective-permute-start.5 = (f32[32,256]{1,0:T(8,128)S(1)}, f32[32,256]{1,0:T(8,128)S(1)}, u32[]{:S(2)}, u32[]{:S(2)}) collective-permute-start(f32[32,256]{1,0:T(8,128)S(1)} %get-tuple-element.17), channel_id=1, source_target_pairs={{0,2},{1,3},{2,0},{3,1},{4,6},{5,7},{6,4},{7,5},{8,10},{9,11},{10,... | collective-permute-start | bytes 98312 | tf_op jit(solution)/shard_map/ppermute | solution.py:251
  17.1 1.4 %copy-start.1 = (f32[1,30,256]{2,0,1:T(1,128)S(1)}, f32[1,30,256]{2,0,1:T(1,128)}, u32[]{:S(2)}) copy-start(f32[1,30,256]{2,0,1:T(1,128)} %param.7) | copy-start | bytes 92164

commit v4 on v3

--- a/solution.py
+++ b/solution.py
@@ -82,12 +82,15 @@
     )
 
 
-def partial_sums(queries, targets):
-    scores = jnp.dot(queries, targets, preferred_element_type=f32)
+def weigh(scores):
     highest = jnp.max(scores, 1, keepdims=True)
     weights = jnp.exp2(scores - highest)
     weights_high = weights.astype(bf16)
     weights_low = (weights - weights_high.astype(f32)).astype(bf16)
+    return highest, weights_high, weights_low
+
+
+def total(highest, weights_high, weights_low, targets):
     values = targets[2 * GROUP : 5 * GROUP]
     along = (((1,), (1,)), ((), ()))
     sums = lax.dot_general(weights_high, values, along, preferred_element_type=f32)
@@ -97,6 +100,27 @@
     return turned[:GROUP] + turned[GROUP : 2 * GROUP] + turned[2 * GROUP : 3 * GROUP]
 
 
+def many_sums(jobs):
+    units = []
+    for n, (queries, targets) in enumerate(jobs):
+        for first in range(0, queries.shape[0], 256):
+            units.append((n, queries[first : first + 256], targets))
+
+    def score(unit):
+        return jnp.dot(unit[1], unit[2], preferred_element_type=f32)
+
+    found = [[] for _ in jobs]
+    upcoming = score(units[0])
+    for k, unit in enumerate(units):
+        scores, upcoming = upcoming, score(units[k + 1]) if k + 1 < len(units) else None
+        found[unit[0]].append(total(*weigh(scores), unit[2]))
+    return [jnp.concatenate(parts, 1) for parts in found]
+
+
+def partial_sums(queries, targets):
+    return many_sums([(queries, targets)])[0]
+
+
 def merged(parts):
     if len(parts) == 1:
         return parts[0]
@@ -110,10 +134,7 @@
     return part / part[GROUP - 2 : GROUP - 1]
 
 
-def usable_cells(counts_ref, positions_ref, which):
-    counts = counts_ref[...].astype(f32)
-    here = lax.broadcasted_iota(jnp.int32, counts.shape, 1) == lax.axis_index("tm")
-    count = jnp.sum(jnp.where(here, counts, 0.0), 1, keepdims=True).astype(jnp.int32)
+def usable_cells(count, positions_ref, which):
     return positions_ref[0:1, :] + which * positions_ref.shape[1] < count
 
 
@@ -135,23 +156,27 @@
 
 
 def fit_first(features, share, counts_ref, positions_ref, block_ref, cells_ref, *refs):
-    parts_ref, queries_ref = refs
+    parts_ref, queries_ref, count_ref = refs
     columns = [
         share_columns(block_ref, features, lax.bitwise_xor(own_cell(), 2 * j), share)
         for j in range(parts_ref.shape[0])
     ]
     queries = query_operand(jnp.concatenate(columns, 1), FIT_SCALE)
     queries_ref[...] = queries
-    usable = usable_cells(counts_ref, positions_ref, own_cell())
+    counts = counts_ref[...].astype(f32).reshape(1, -1)
+    here = lax.broadcasted_iota(jnp.int32, counts.shape, 1) == lax.axis_index("tm")
+    count = jnp.sum(jnp.where(here, counts, 0.0), 1, keepdims=True).astype(jnp.int32)
+    count_ref[...] = jnp.broadcast_to(count, count_ref.shape)
+    usable = usable_cells(count, positions_ref, own_cell())
     targets = target_operand(whole(cells_ref, features), FIT_SCALE, usable)
     parts = partial_sums(queries, targets)
     for j in range(parts_ref.shape[0]):
         parts_ref[j] = parts[:, j * share : (j + 1) * share]
 
 
-def fit_second(features, share, counts_ref, positions_ref, queries_ref, parts_ref, *refs):
+def fit_second(features, share, count_ref, positions_ref, queries_ref, parts_ref, *refs):
     cells_ref, operand_ref, *fit_refs = refs
-    usable = usable_cells(counts_ref, positions_ref, lax.bitwise_xor(own_cell(), 1))
+    usable = usable_cells(count_ref[0:1, 0:1], positions_ref, lax.bitwise_xor(own_cell(), 1))
     targets = target_operand(whole(cells_ref, features), FIT_SCALE, usable)
     operand_ref[...] = targets
     parts = partial_sums(queries_ref[share:, :], targets)
@@ -161,7 +186,7 @@
 
 def bridge(queries, key_refs, features):
     targets = [target_operand(whole(ref, features), BRIDGE_SCALE) for ref in key_refs]
-    return merged([partial_sums(queries, target) for target in targets])
+    return merged(many_sums([(queries, target) for target in targets]))
 
 
 def own_near(features, share, block_ref, fit_queries_ref, parts_ref, operand_ref, *refs):
@@ -268,20 +293,20 @@
     operand = jax.ShapeDtypeStruct((6 * GROUP, width), bf16)
     own_queries = jax.ShapeDtypeStruct((share, 6 * GROUP), bf16)
     positions = call(number_cells, jax.ShapeDtypeStruct((8, width), jnp.int32), (), 10**10)
-    counts = cell_counts[None]
-    parts, fit_queries = call(
+    parts, fit_queries, count = call(
         functools.partial(fit_first, features, share),
         (
             jax.ShapeDtypeStruct((shares, GROUP, share), f32),
             jax.ShapeDtypeStruct((shares * share, 6 * GROUP), bf16),
+            jax.ShapeDtypeStruct((8, LANES), jnp.int32),
         ),
-        (counts, positions, block, cells),
+        (cell_counts, positions, block, cells),
         10**9,
     )
     near_operand, *sent_fits = call(
         functools.partial(fit_second, features, share),
         (operand,) + (part,) * (shares - 1),
-        (counts, positions, fit_queries, parts, near_cells),
+        (count, positions, fit_queries, parts, near_cells),
         10**9,
     )
     fits = [over_cell(x, 2 * by) for by, x in zip(range(1, shares), sent_fits)]

time: 19.4 us -> 18.9 us (0.974)
  waiting for transfers between devices: 1.34 us -> 2.38 us
  Pallas kernels: 7.34 us -> 6.43 us
  local copies, waits for them, and re-layouts: 0.65 us -> 0.02 us
    ppermute x2, waiting for transfers between devices: 1.33 us -> 2.37 us  [over_cell(): return lax.ppermute(x, 'cell', [(c, c ^ by) for c in range(cell_size)])]
    pallas_call x6, Pallas kernels: 7.34 us -> 6.43 us  [call(): pl.pallas_call(kernel, out_shape=out_shape, in_specs=[VMEM] * len(args),...]
    unnamed x8, local copies, waits for them, and re-layouts: 0.65 us -> 0.02 us
  transfers between devices with their start and end apart: 6 -> 6, of which waited for: 1 -> 1; matrix products, arithmetic and copies ran while one was open for 0% -> 0% of each run, Pallas kernels for 34% -> 31%
where the time goes in v4:
time: 18.9 us; the launch traced here: 18.7 us
  starting transfers between devices  9.18 us (49%)
  Pallas kernels  6.43 us (34%)
  waiting for transfers between devices  2.38 us (13%)
  between operations  0.72 us (4%)
    pallas_call x6, Pallas kernels, call(): pl.pallas_call(kernel, out_shape=out_shape, in_specs=[VMEM] * len(args),...  6.43 us
    ppermute x2, starting transfers between devices, over_cell(): return lax.ppermute(x, 'cell', [(c, c ^ by) for c in range(cell_size)])  4.79 us
    ppermute x4, starting transfers between devices, over_time(): lax.ppermute(block, ('tm', 'particle'), [(t * blocks + p, pair(t, times)...  4.4 us
    ppermute x2, waiting for transfers between devices, over_cell(): return lax.ppermute(x, 'cell', [(c, c ^ by) for c in range(cell_size)])  2.37 us
  transfers between devices with their start and end apart: 6, of which 1 were waited for; matrix products, arithmetic and copies ran while one was open for 0% of the time, Pallas kernels for 31%

profile of v4, /device:TPU:0, one launch (start us, length us, event | category | flops | bytes accessed | tf_op | source)
XLA Modules:
  0.0 18.7 jit_solution(3495034682872497946)
XLA Ops:
  0.6 0.6 %collective-permute-start.1 = (f32[240,128]{1,0:T(8,128)}, f32[240,128]{1,0:T(8,128)S(1)}, u32[]{:S(2)}, u32[]{:S(2)}) collective-permute-start(f32[240,128]{1,0:T(8,128)} %bitcast.5), channel_id=1, source_target_pairs={{0,8},{4,12},{8,0},{12,4},{16,24},{20,28},{24,16},{28,20},{1,9},{5... | collective-permute-start | bytes 368648 | tf_op jit(solution)/shard_map/ppermute | solution.py:280
  1.2 2.6 %collective-permute-start.2 = (f32[240,128]{1,0:T(8,128)}, f32[240,128]{1,0:T(8,128)S(1)}, u32[]{:S(2)}, u32[]{:S(2)}) collective-permute-start(f32[240,128]{1,0:T(8,128)} %bitcast.6), channel_id=1, source_target_pairs={{0,12},{4,8},{8,4},{12,0},{16,28},{20,24},{24,20},{28,16},{1,13},{... | collective-permute-start | bytes 368648 | tf_op jit(solution)/shard_map/ppermute | solution.py:280
  3.8 1.2 %collective-permute-start.3 = (f32[240,128]{1,0:T(8,128)}, f32[240,128]{1,0:T(8,128)S(1)}, u32[]{:S(2)}, u32[]{:S(2)}) collective-permute-start(f32[240,128]{1,0:T(8,128)} %bitcast.7), channel_id=1, source_target_pairs={{0,24},{4,28},{8,16},{12,20},{16,8},{20,12},{24,0},{28,4},{1,25},{... | collective-permute-start | bytes 368648 | tf_op jit(solution)/shard_map/ppermute | solution.py:280
  5.0 0.0 collective-permute-start.4
  5.0 0.0 copy-start
  5.0 0.0 copy-start.2
  5.0 2.0 %collective-permute-start = (f32[240,128]{1,0:T(8,128)}, f32[240,128]{1,0:T(8,128)S(1)}, u32[]{:S(2)}, u32[]{:S(2)}) collective-permute-start(f32[240,128]{1,0:T(8,128)} %bitcast.13), channel_id=1, source_target_pairs={{0,1},{1,0},{2,3},{3,2},{4,5},{5,4},{6,7},{7,6},{8,9},{9,8},{10,11... | collective-permute-start | bytes 368648 | tf_op jit(solution)/shard_map/ppermute | solution.py:276
  7.1 0.0 copy-done
  7.1 0.0 copy-done.2
  7.1 0.0 copy-done.3
  7.1 1.4 %shard_map.60 = (f32[2,32,256]{2,1,0:T(8,128)S(1)}, bf16[512,192]{1,0:T(8,128)(2,1)S(1)}, s32[8,128]{1,0:T(8,128)S(1)}) custom-call(s32[4]{0:T(128)S(1)} %copy-done.3, s32[8,1024]{1,0:T(8,128)S(1)} %shard_map.59.positions_ref, f32[240,128]{1,0:T(8,128)S(1)} %bitcast.9, f32[240,128]{1,0:T(8,128)S(1)} %bitcast.14), custom_call_target="tpu_custom_call" | custom-call | flops 1000000000 | bytes 278544 | tf_op jit(solution)/shard_map/pallas_call | solution.py:244
  8.6 2.4 %collective-permute-done.refs_0_ = f32[240,128]{1,0:T(8,128)S(1)} collective-permute-done((f32[240,128]{1,0:T(8,128)}, f32[240,128]{1,0:T(8,128)S(1)}, u32[]{:S(2)}, u32[]{:S(2)}) %collective-permute-start) | collective-permute-done | bytes 122912 | tf_op jit(solution)/shard_map/ppermute | solution.py:276
  10.9 1.1 %shard_map.61 = (bf16[192,1024]{1,0:T(8,128)(2,1)S(1)}, f32[32,256]{1,0:T(8,128)S(1)}) custom-call(s32[8,128]{1,0:T(8,128)S(1)} %get-tuple-element.14.count_ref, s32[8,1024]{1,0:T(8,128)S(1)} %shard_map.59.positions_ref, bf16[512,192]{1,0:T(8,128)(2,1)S(1)} %get-tuple-element.12.queries_ref.fit_queries_ref, f32[2,32,256]{2,1,0:T(8,128)S(1)} %get-tuple-element.13.parts_ref, ...), custom_call_target="tpu_custom_call" | custom-call | flops 1000000000 | bytes 618496 | tf_op jit(solution)/shard_map/pallas_call | solution.py:244
  12.1 2.7 %collective-permute-start.5 = (f32[32,256]{1,0:T(8,128)S(1)}, f32[32,256]{1,0:T(8,128)S(1)}, u32[]{:S(2)}, u32[]{:S(2)}) collective-permute-start(f32[32,256]{1,0:T(8,128)S(1)} %get-tuple-element.19), channel_id=1, source_target_pairs={{0,2},{1,3},{2,0},{3,1},{4,6},{5,7},{6,4},{7,5},{8,10},{9,11},{10,... | collective-permute-start | bytes 98312 | tf_op jit(solution)/shard_map/ppermute | solution.py:276
  14.8 0.0 collective-permute-done.1.refs_0_
  14.8 0.0 collective-permute-done.2.refs_1_
  14.8 1.7 %shard_map.62 = (f32[32,256]{1,0:T(8,128)S(1)}, f32[32,256]{1,0:T(8,128)S(1)}, bf16[256,192]{1,0:T(8,128)(2,1)S(1)}) custom-call(f32[240,128]{1,0:T(8,128)S(1)} %bitcast.10, bf16[512,192]{1,0:T(8,128)(2,1)S(1)} %get-tuple-element.12.queries_ref.fit_queries_ref, f32[2,32,256]{2,1,0:T(8,128)S(1)} %get-tuple-element.13.parts_ref, ...), custom_call_target="tpu_custom_call" | custom-call | flops 1000000000 | bytes 1613824 | tf_op jit(solution)/shard_map/pallas_call | solution.py:244
  16.6 0.0 collective-permute-done.3.refs_0_
  16.6 0.0 collective-permute-done.4.refs_1_
  16.6 0.0 copy-start.1
  16.6 1.4 %shard_map.63.far_ref = f32[32,256]{1,0:T(8,128)S(1)} custom-call(bf16[256,192]{1,0:T(8,128)(2,1)S(1)} %get-tuple-element.17.queries_ref, f32[240,128]{1,0:T(8,128)S(1)} %collective-permute-done.3.refs_0_, f32[240,128]{1,0:T(8,128)S(1)} %collective-permute-done.4.refs_1_), custom_call_target="tpu_custom_call" | custom-call | flops 1000000000 | bytes 442368 | tf_op jit(solution)/shard_map/pallas_call | solution.py:244
  18.0 0.0 collective-permute-done.5.refs_1_
  18.0 0.0 copy-done.1
  18.0 0.7 %shard_map.64 = (f32[30,1,256]{2,1,0:T(1,128)}, f32[30,1,256]{2,1,0:T(1,128)}) custom-call(f32[240,128]{1,0:T(8,128)S(1)} %bitcast.11, f32[30,1,256]{2,1,0:T(1,128)S(1)} %bitcast.12, f32[32,256]{1,0:T(8,128)S(1)} %get-tuple-element.16.near_ref, f32[32,256]{1,0:T(8,128)S(1)} %shard_map.63.far_ref, f32[32,256]{1,0:T(8,128)S(1)} %get-tuple-element.18.refs_0_, ...), custom_call_target="tpu_custom_call" | custom-call | flops 1000000 | bytes 284672 | tf_op jit(solution)/shard_map/pallas_call | solution.py:244
  (2 shorter events, 0.0 us)
Async XLA Ops:
  0.6 14.2 %collective-permute-start.1 = (f32[240,128]{1,0:T(8,128)}, f32[240,128]{1,0:T(8,128)S(1)}, u32[]{:S(2)}, u32[]{:S(2)}) collective-permute-start(f32[240,128]{1,0:T(8,128)} %bitcast.5), channel_id=1, source_target_pairs={{0,8},{4,12},{8,0},{12,4},{16,24},{20,28},{24,16},{28,20},{1,9},{5... | collective-permute-start | bytes 368648 | tf_op jit(solution)/shard_map/ppermute | solution.py:280
  1.2 13.6 %collective-permute-start.2 = (f32[240,128]{1,0:T(8,128)}, f32[240,128]{1,0:T(8,128)S(1)}, u32[]{:S(2)}, u32[]{:S(2)}) collective-permute-start(f32[240,128]{1,0:T(8,128)} %bitcast.6), channel_id=1, source_target_pairs={{0,12},{4,8},{8,4},{12,0},{16,28},{20,24},{24,20},{28,16},{1,13},{... | collective-permute-start | bytes 368648 | tf_op jit(solution)/shard_map/ppermute | solution.py:280
  3.8 12.8 %collective-permute-start.3 = (f32[240,128]{1,0:T(8,128)}, f32[240,128]{1,0:T(8,128)S(1)}, u32[]{:S(2)}, u32[]{:S(2)}) collective-permute-start(f32[240,128]{1,0:T(8,128)} %bitcast.7), channel_id=1, source_target_pairs={{0,24},{4,28},{8,16},{12,20},{16,8},{20,12},{24,0},{28,4},{1,25},{... | collective-permute-start | bytes 368648 | tf_op jit(solution)/shard_map/ppermute | solution.py:280
  5.0 11.6 %collective-permute-start.4 = (f32[240,128]{1,0:T(8,128)}, f32[240,128]{1,0:T(8,128)S(1)}, u32[]{:S(2)}, u32[]{:S(2)}) collective-permute-start(f32[240,128]{1,0:T(8,128)} %bitcast.8), channel_id=1, source_target_pairs={{0,28},{4,24},{8,20},{12,16},{16,12},{20,8},{24,4},{28,0},{1,29},{... | collective-permute-start | bytes 368648 | tf_op jit(solution)/shard_map/ppermute | solution.py:280
  5.0 2.1 %copy-start = (f32[1,30,1024]{2,0,1:T(1,128)S(1)}, f32[1,30,1024]{2,0,1:T(1,128)}, u32[]{:S(2)}) copy-start(f32[1,30,1024]{2,0,1:T(1,128)} %param.4) | copy-start | bytes 368644
  5.0 2.1 %copy-start.2 = (f32[1,30,1024]{2,0,1:T(1,128)S(1)}, f32[1,30,1024]{2,0,1:T(1,128)}, u32[]{:S(2)}) copy-start(f32[1,30,1024]{2,0,1:T(1,128)} %param.5) | copy-start | bytes 368644
  5.0 2.1 %copy-start.3 = (s32[4]{0:T(128)S(1)}, s32[4]{0:T(128)}, u32[]{:S(2)}) copy-start(s32[4]{0:T(128)} %counts_ref.1) | copy-start | bytes 52
  5.0 5.9 %collective-permute-start = (f32[240,128]{1,0:T(8,128)}, f32[240,128]{1,0:T(8,128)S(1)}, u32[]{:S(2)}, u32[]{:S(2)}) collective-permute-start(f32[240,128]{1,0:T(8,128)} %bitcast.13), channel_id=1, source_target_pairs={{0,1},{1,0},{2,3},{3,2},{4,5},{5,4},{6,7},{7,6},{8,9},{9,8},{10,11... | collective-permute-start | bytes 368648 | tf_op jit(solution)/shard_map/ppermute | solution.py:276
  12.1 5.9 %collective-permute-start.5 = (f32[32,256]{1,0:T(8,128)S(1)}, f32[32,256]{1,0:T(8,128)S(1)}, u32[]{:S(2)}, u32[]{:S(2)}) collective-permute-start(f32[32,256]{1,0:T(8,128)S(1)} %get-tuple-element.19), channel_id=1, source_target_pairs={{0,2},{1,3},{2,0},{3,1},{4,6},{5,7},{6,4},{7,5},{8,10},{9,11},{10,... | collective-permute-start | bytes 98312 | tf_op jit(solution)/shard_map/ppermute | solution.py:276
  16.6 1.4 %copy-start.1 = (f32[1,30,256]{2,0,1:T(1,128)S(1)}, f32[1,30,256]{2,0,1:T(1,128)}, u32[]{:S(2)}) copy-start(f32[1,30,256]{2,0,1:T(1,128)} %param.7) | copy-start | bytes 92164

commit v5 on v4

--- a/solution.py
+++ b/solution.py
@@ -100,20 +100,21 @@
     return turned[:GROUP] + turned[GROUP : 2 * GROUP] + turned[2 * GROUP : 3 * GROUP]
 
 
-def many_sums(jobs):
+def many_sums(jobs, block=256, ahead=1):
     units = []
     for n, (queries, targets) in enumerate(jobs):
-        for first in range(0, queries.shape[0], 256):
-            units.append((n, queries[first : first + 256], targets))
+        for first in range(0, queries.shape[0], block):
+            units.append((n, queries[first : first + block], targets))
 
     def score(unit):
         return jnp.dot(unit[1], unit[2], preferred_element_type=f32)
 
     found = [[] for _ in jobs]
-    upcoming = score(units[0])
+    scored = [score(unit) for unit in units[:ahead]]
     for k, unit in enumerate(units):
-        scores, upcoming = upcoming, score(units[k + 1]) if k + 1 < len(units) else None
-        found[unit[0]].append(total(*weigh(scores), unit[2]))
+        if k + ahead < len(units):
+            scored.append(score(units[k + ahead]))
+        found[unit[0]].append(total(*weigh(scored[k]), unit[2]))
     return [jnp.concatenate(parts, 1) for parts in found]
 
 
@@ -179,7 +180,7 @@
     usable = usable_cells(count_ref[0:1, 0:1], positions_ref, lax.bitwise_xor(own_cell(), 1))
     targets = target_operand(whole(cells_ref, features), FIT_SCALE, usable)
     operand_ref[...] = targets
-    parts = partial_sums(queries_ref[share:, :], targets)
+    parts = many_sums([(queries_ref[share:, :], targets)], 128, 0)[0]
     for j, fit_ref in enumerate(fit_refs):
         fit_ref[...] = merged([parts_ref[j + 1], parts[:, j * share : (j + 1) * share]])
 
@@ -189,17 +190,56 @@
     return merged(many_sums([(queries, target) for target in targets]))
 
 
-def own_near(features, share, block_ref, fit_queries_ref, parts_ref, operand_ref, *refs):
+def has_far_side():
+    time = lax.axis_index("tm")
+    other = time - 1 + 2 * lax.rem(time, 2)
+    return jnp.logical_and(other >= 0, other < lax.axis_size("tm"))
+
+
+def goes_early():
+    return jnp.logical_and(own_cell() < lax.axis_size("cell") // 2, has_far_side())
+
+
+def own_fit(share, queries_ref, parts_ref, operand_ref):
+    return merged([parts_ref[0], partial_sums(queries_ref[:share, :], operand_ref[...])])
+
+
+def own_early(share, queries_ref, parts_ref, operand_ref, fit_ref):
+    @pl.when(goes_early())
+    def _():
+        fit_ref[...] = own_fit(share, queries_ref, parts_ref, operand_ref)
+
+    @pl.when(jnp.logical_not(goes_early()))
+    def _():
+        fit_ref[...] = jnp.zeros_like(fit_ref)
+
+
+def own_near(features, share, block_ref, early_ref, fit_queries_ref, parts_ref, operand_ref, *refs):
     *key_refs, fit_ref, pull_ref, queries_ref = refs
-    fit_ref[...] = merged([parts_ref[0], partial_sums(fit_queries_ref[:share, :], operand_ref[...])])
     queries = query_operand(share_columns(block_ref, features, own_cell(), share), BRIDGE_SCALE)
     queries_ref[...] = queries
-    pull_ref[...] = bridge(queries, key_refs, features)
+
+    @pl.when(goes_early())
+    def _():
+        fit_ref[...] = early_ref[...]
+        pull_ref[...] = bridge(queries_ref[...], key_refs, features)
+
+    @pl.when(jnp.logical_not(goes_early()))
+    def _():
+        fit_ref[...] = own_fit(share, fit_queries_ref, parts_ref, operand_ref)
+        pull_ref[...] = bridge(queries_ref[...], key_refs, features)
 
 
 def own_far(features, queries_ref, *refs):
     *key_refs, pull_ref = refs
-    pull_ref[...] = bridge(queries_ref[...], key_refs, features)
+
+    @pl.when(has_far_side())
+    def _():
+        pull_ref[...] = bridge(queries_ref[...], key_refs, features)
+
+    @pl.when(jnp.logical_not(has_far_side()))
+    def _():
+        pull_ref[...] = jnp.ones_like(pull_ref)
 
 
 def finish(features, share, block_ref, noise_ref, near_ref, far_ref, *refs):
@@ -309,11 +349,14 @@
         (count, positions, fit_queries, parts, near_cells),
         10**9,
     )
+    early_fit = call(
+        functools.partial(own_early, share), part, (fit_queries, parts, near_operand), 10**9
+    )
     fits = [over_cell(x, 2 * by) for by, x in zip(range(1, shares), sent_fits)]
     own_fit, near_pull, bridge_queries = call(
         functools.partial(own_near, features, share),
         (part, part, own_queries),
-        (block, fit_queries, parts, near_operand, *keys["near"]),
+        (block, early_fit, fit_queries, parts, near_operand, *keys["near"]),
         10**9,
     )
     far_pull = call(

time: 18.9 us -> 18.2 us (0.963)
  Pallas kernels: 6.43 us -> 5 us
  local copies, waits for them, and re-layouts: 0.02 us -> 0.52 us
  waiting for transfers between devices: 2.38 us -> 2.58 us
    pallas_call x6 -> x7, Pallas kernels: 6.43 us -> 5 us  [call(): pl.pallas_call(kernel, out_shape=out_shape, in_specs=[VMEM] * len(args),...]
    unnamed x8, local copies, waits for them, and re-layouts: 0.02 us -> 0.52 us
    ppermute x2, waiting for transfers between devices: 2.37 us -> 2.57 us  [over_cell(): return lax.ppermute(x, 'cell', [(c, c ^ by) for c in range(cell_size)])]
  transfers between devices with their start and end apart: 6 -> 6, of which waited for: 1 -> 2; matrix products, arithmetic and copies ran while one was open for 0% -> 0% of each run, Pallas kernels for 31% -> 24%
where the time goes in v5:
time: 18.2 us; the launch traced here: 18 us
  starting transfers between devices  9.18 us (50%)
  Pallas kernels  5 us (27%)
  waiting for transfers between devices  2.58 us (14%)
  between operations  0.71 us (4%)
  local copies, waits for them, and re-layouts  0.52 us (3%)
    pallas_call x7, Pallas kernels, call(): pl.pallas_call(kernel, out_shape=out_shape, in_specs=[VMEM] * len(args),...  5 us
    ppermute x2, starting transfers between devices, over_cell(): return lax.ppermute(x, 'cell', [(c, c ^ by) for c in range(cell_size)])  4.79 us
    ppermute x4, starting transfers between devices, over_time(): lax.ppermute(block, ('tm', 'particle'), [(t * blocks + p, pair(t, times)...  4.4 us
    ppermute x2, waiting for transfers between devices, over_cell(): return lax.ppermute(x, 'cell', [(c, c ^ by) for c in range(cell_size)])  2.57 us
    unnamed x8, local copies, waits for them, and re-layouts  0.52 us
  transfers between devices with their start and end apart: 6, of which 2 were waited for; matrix products, arithmetic and copies ran while one was open for 0% of the time, Pallas kernels for 24%

profile of v5, /device:TPU:0, one launch (start us, length us, event | category | flops | bytes accessed | tf_op | source)
XLA Modules:
  0.0 18.0 jit_solution(14391023866029597167)
XLA Ops:
  0.6 0.6 %collective-permute-start.1 = (f32[240,128]{1,0:T(8,128)}, f32[240,128]{1,0:T(8,128)S(1)}, u32[]{:S(2)}, u32[]{:S(2)}) collective-permute-start(f32[240,128]{1,0:T(8,128)} %bitcast.5), channel_id=1, source_target_pairs={{0,8},{4,12},{8,0},{12,4},{16,24},{20,28},{24,16},{28,20},{1,9},{5... | collective-permute-start | bytes 368648 | tf_op jit(solution)/shard_map/ppermute | solution.py:320
  1.2 2.6 %collective-permute-start.2 = (f32[240,128]{1,0:T(8,128)}, f32[240,128]{1,0:T(8,128)S(1)}, u32[]{:S(2)}, u32[]{:S(2)}) collective-permute-start(f32[240,128]{1,0:T(8,128)} %bitcast.6), channel_id=1, source_target_pairs={{0,12},{4,8},{8,4},{12,0},{16,28},{20,24},{24,20},{28,16},{1,13},{... | collective-permute-start | bytes 368648 | tf_op jit(solution)/shard_map/ppermute | solution.py:320
  3.8 1.2 %collective-permute-start.3 = (f32[240,128]{1,0:T(8,128)}, f32[240,128]{1,0:T(8,128)S(1)}, u32[]{:S(2)}, u32[]{:S(2)}) collective-permute-start(f32[240,128]{1,0:T(8,128)} %bitcast.7), channel_id=1, source_target_pairs={{0,24},{4,28},{8,16},{12,20},{16,8},{20,12},{24,0},{28,4},{1,25},{... | collective-permute-start | bytes 368648 | tf_op jit(solution)/shard_map/ppermute | solution.py:320
  5.0 0.0 collective-permute-start.4
  5.0 0.0 copy-start
  5.0 0.0 copy-start.2
  5.0 0.0 copy-start.3
  5.0 2.0 %collective-permute-start = (f32[240,128]{1,0:T(8,128)}, f32[240,128]{1,0:T(8,128)S(1)}, u32[]{:S(2)}, u32[]{:S(2)}) collective-permute-start(f32[240,128]{1,0:T(8,128)} %bitcast.13), channel_id=1, source_target_pairs={{0,1},{1,0},{2,3},{3,2},{4,5},{5,4},{6,7},{7,6},{8,9},{9,8},{10,11... | collective-permute-start | bytes 368648 | tf_op jit(solution)/shard_map/ppermute | solution.py:316
  7.1 0.0 copy-done
  7.1 0.0 copy-done.2
  7.1 0.0 copy-done.3
  7.1 1.4 %shard_map.60 = (f32[2,32,256]{2,1,0:T(8,128)S(1)}, bf16[512,192]{1,0:T(8,128)(2,1)S(1)}, s32[8,128]{1,0:T(8,128)S(1)}) custom-call(s32[4]{0:T(128)S(1)} %copy-done.3, s32[8,1024]{1,0:T(8,128)S(1)} %shard_map.59.positions_ref, f32[240,128]{1,0:T(8,128)S(1)} %bitcast.9, f32[240,128]{1,0:T(8,128)S(1)} %bitcast.14), custom_call_target="tpu_custom_call" | custom-call | flops 1000000000 | bytes 278544 | tf_op jit(solution)/shard_map/pallas_call | solution.py:284
  8.6 2.4 %collective-permute-done.refs_0_ = f32[240,128]{1,0:T(8,128)S(1)} collective-permute-done((f32[240,128]{1,0:T(8,128)}, f32[240,128]{1,0:T(8,128)S(1)}, u32[]{:S(2)}, u32[]{:S(2)}) %collective-permute-start) | collective-permute-done | bytes 122912 | tf_op jit(solution)/shard_map/ppermute | solution.py:316
  10.9 0.9 %shard_map.61 = (bf16[192,1024]{1,0:T(8,128)(2,1)S(1)}, f32[32,256]{1,0:T(8,128)S(1)}) custom-call(s32[8,128]{1,0:T(8,128)S(1)} %get-tuple-element.14.count_ref, s32[8,1024]{1,0:T(8,128)S(1)} %shard_map.59.positions_ref, bf16[512,192]{1,0:T(8,128)(2,1)S(1)} %get-tuple-element.12.queries_ref.fit_queries_ref, f32[2,32,256]{2,1,0:T(8,128)S(1)} %get-tuple-element.13.parts_ref, ...), custom_call_target="tpu_custom_call" | custom-call | flops 1000000000 | bytes 618496 | tf_op jit(solution)/shard_map/pallas_call | solution.py:284
  11.9 2.7 %collective-permute-start.5 = (f32[32,256]{1,0:T(8,128)S(1)}, f32[32,256]{1,0:T(8,128)S(1)}, u32[]{:S(2)}, u32[]{:S(2)}) collective-permute-start(f32[32,256]{1,0:T(8,128)S(1)} %get-tuple-element.19), channel_id=1, source_target_pairs={{0,2},{1,3},{2,0},{3,1},{4,6},{5,7},{6,4},{7,5},{8,10},{9,11},{10,... | collective-permute-start | bytes 98312 | tf_op jit(solution)/shard_map/ppermute | solution.py:316
  14.6 0.0 collective-permute-done.1.refs_0_
  14.6 0.0 collective-permute-done.2.refs_1_
  14.7 1.9 %shard_map.63 = (f32[32,256]{1,0:T(8,128)S(1)}, f32[32,256]{1,0:T(8,128)S(1)}, bf16[256,192]{1,0:T(8,128)(2,1)S(1)}) custom-call(f32[240,128]{1,0:T(8,128)S(1)} %bitcast.10, f32[32,256]{1,0:T(8,128)S(1)} %shard_map.62.early_ref, bf16[512,192]{1,0:T(8,128)(2,1)S(1)} %get-tuple-element.12.queries_ref.fit_queries_ref, ...), custom_call_target="tpu_custom_call" | custom-call | flops 1000000000 | bytes 1646592 | tf_op jit(solution)/shard_map/pallas_call | solution.py:284
  16.5 0.0 collective-permute-done.3.refs_0_
  16.5 0.0 collective-permute-done.4.refs_1_
  16.5 0.0 copy-start.1
  16.6 0.2 %collective-permute-done.5.refs_1_ = f32[32,256]{1,0:T(8,128)S(1)} collective-permute-done((f32[32,256]{1,0:T(8,128)S(1)}, f32[32,256]{1,0:T(8,128)S(1)}, u32[]{:S(2)}, u32[]{:S(2)}) %collective-permute-start.5) | collective-permute-done | bytes 32800 | tf_op jit(solution)/shard_map/ppermute | solution.py:316
  16.8 0.5 %copy-done.1 = f32[1,30,256]{2,0,1:T(1,128)S(1)} copy-done((f32[1,30,256]{2,0,1:T(1,128)S(1)}, f32[1,30,256]{2,0,1:T(1,128)}, u32[]{:S(2)}) %copy-start.1) | copy-done | bytes 30744
  17.3 0.7 %shard_map.65 = (f32[30,1,256]{2,1,0:T(1,128)}, f32[30,1,256]{2,1,0:T(1,128)}) custom-call(f32[240,128]{1,0:T(8,128)S(1)} %bitcast.11, f32[30,1,256]{2,1,0:T(1,128)S(1)} %bitcast.12, f32[32,256]{1,0:T(8,128)S(1)} %get-tuple-element.16.near_ref, f32[32,256]{1,0:T(8,128)S(1)} %shard_map.64.far_ref, f32[32,256]{1,0:T(8,128)S(1)} %get-tuple-element.18.refs_0_, ...), custom_call_target="tpu_custom_call" | custom-call | flops 1000000 | bytes 284672 | tf_op jit(solution)/shard_map/pallas_call | solution.py:284
  (3 shorter events, 0.1 us)
Async XLA Ops:
  0.6 14.0 %collective-permute-start.1 = (f32[240,128]{1,0:T(8,128)}, f32[240,128]{1,0:T(8,128)S(1)}, u32[]{:S(2)}, u32[]{:S(2)}) collective-permute-start(f32[240,128]{1,0:T(8,128)} %bitcast.5), channel_id=1, source_target_pairs={{0,8},{4,12},{8,0},{12,4},{16,24},{20,28},{24,16},{28,20},{1,9},{5... | collective-permute-start | bytes 368648 | tf_op jit(solution)/shard_map/ppermute | solution.py:320
  1.2 13.5 %collective-permute-start.2 = (f32[240,128]{1,0:T(8,128)}, f32[240,128]{1,0:T(8,128)S(1)}, u32[]{:S(2)}, u32[]{:S(2)}) collective-permute-start(f32[240,128]{1,0:T(8,128)} %bitcast.6), channel_id=1, source_target_pairs={{0,12},{4,8},{8,4},{12,0},{16,28},{20,24},{24,20},{28,16},{1,13},{... | collective-permute-start | bytes 368648 | tf_op jit(solution)/shard_map/ppermute | solution.py:320
  3.8 12.7 %collective-permute-start.3 = (f32[240,128]{1,0:T(8,128)}, f32[240,128]{1,0:T(8,128)S(1)}, u32[]{:S(2)}, u32[]{:S(2)}) collective-permute-start(f32[240,128]{1,0:T(8,128)} %bitcast.7), channel_id=1, source_target_pairs={{0,24},{4,28},{8,16},{12,20},{16,8},{20,12},{24,0},{28,4},{1,25},{... | collective-permute-start | bytes 368648 | tf_op jit(solution)/shard_map/ppermute | solution.py:320
  5.0 11.5 %collective-permute-start.4 = (f32[240,128]{1,0:T(8,128)}, f32[240,128]{1,0:T(8,128)S(1)}, u32[]{:S(2)}, u32[]{:S(2)}) collective-permute-start(f32[240,128]{1,0:T(8,128)} %bitcast.8), channel_id=1, source_target_pairs={{0,28},{4,24},{8,20},{12,16},{16,12},{20,8},{24,4},{28,0},{1,29},{... | collective-permute-start | bytes 368648 | tf_op jit(solution)/shard_map/ppermute | solution.py:320
  5.0 2.1 %copy-start = (f32[1,30,1024]{2,0,1:T(1,128)S(1)}, f32[1,30,1024]{2,0,1:T(1,128)}, u32[]{:S(2)}) copy-start(f32[1,30,1024]{2,0,1:T(1,128)} %param.4) | copy-start | bytes 368644
  5.0 2.1 %copy-start.2 = (f32[1,30,1024]{2,0,1:T(1,128)S(1)}, f32[1,30,1024]{2,0,1:T(1,128)}, u32[]{:S(2)}) copy-start(f32[1,30,1024]{2,0,1:T(1,128)} %param.5) | copy-start | bytes 368644
  5.0 2.1 %copy-start.3 = (s32[4]{0:T(128)S(1)}, s32[4]{0:T(128)}, u32[]{:S(2)}) copy-start(s32[4]{0:T(128)} %counts_ref.1) | copy-start | bytes 52
  5.0 5.9 %collective-permute-start = (f32[240,128]{1,0:T(8,128)}, f32[240,128]{1,0:T(8,128)S(1)}, u32[]{:S(2)}, u32[]{:S(2)}) collective-permute-start(f32[240,128]{1,0:T(8,128)} %bitcast.13), channel_id=1, source_target_pairs={{0,1},{1,0},{2,3},{3,2},{4,5},{5,4},{6,7},{7,6},{8,9},{9,8},{10,11... | collective-permute-start | bytes 368648 | tf_op jit(solution)/shard_map/ppermute | solution.py:316
  11.9 4.9 %collective-permute-start.5 = (f32[32,256]{1,0:T(8,128)S(1)}, f32[32,256]{1,0:T(8,128)S(1)}, u32[]{:S(2)}, u32[]{:S(2)}) collective-permute-start(f32[32,256]{1,0:T(8,128)S(1)} %get-tuple-element.19), channel_id=1, source_target_pairs={{0,2},{1,3},{2,0},{3,1},{4,6},{5,7},{6,4},{7,5},{8,10},{9,11},{10,... | collective-permute-start | bytes 98312 | tf_op jit(solution)/shard_map/ppermute | solution.py:316
  16.5 0.8 %copy-start.1 = (f32[1,30,256]{2,0,1:T(1,128)S(1)}, f32[1,30,256]{2,0,1:T(1,128)}, u32[]{:S(2)}) copy-start(f32[1,30,256]{2,0,1:T(1,128)} %param.7) | copy-start | bytes 92164
